TPU v7x, 256 devices: a whole 4x4x8 slice. The times are simulated.
256 devices in a mesh: site: 8 (over y, core), sector: 32 (over z, x).
Axes of the slice: x: 4, y: 4, z: 8, core: 2. Of those that a mesh axis runs over, the one named last changes fastest.
Arguments:
- env_in: bfloat16 [256, 20, 1024], P('sector'), as said below
- mpo_terms: bfloat16 [4, 20, 20], replicated, may hold values from -1.25 to 1.25
- site_tensors: bfloat16 [8, 256, 4, 1024], P('site', 'sector'), may hold values from -0.75 to 0.75
- route_owner: int32 [8, 256, 4, 1], P('site'), may hold values from 0 to 31; in each aligned block of 32 rows (0 to 31, 32 to 63, ..., all dimensions but the last counted through in order) at most 2 rows name the same one
- route_sector: int32 [8, 256, 4], P('site'), may hold values from 0 to 7
- live_block_extent: int32 [256], P('sector'), may hold values from 8 to 32, as said below
- psi: bfloat16 [8, 256, 1024], P('site', 'sector'), may hold values from -6 to 6
- right_env: bfloat16 [8, 256, 20, 1024], P('site', 'sector'), as said below
Outputs:
- ground: float32 [8, 256, 1024], P('site', 'sector')
- site_energy: float32 [8], P('site')
Inputs may be any that keep to these rules, and one draw needn't show every extreme that they name: `route_owner`: among the rows of one device at one site (8 sectors times 4 states) no owner is named more than 2 times, and some device's rows name one owner exactly 2 times. `live_block_extent`: some sector block is full in every draw. `env_in`: each block is symmetric in its two block indices for every bond index. `right_env`: each block is symmetric in its two block indices for every bond index.
All inputs are finite; a program needn't handle non-finite values.
Results may differ from a plain program's by a relative error of at most 0.03.
Values may be sent and summed in bfloat16 or wider, within the bound.
No kernel may reach another device: no remote copies, remote signals or barrier semaphores. Data moves between devices by JAX's collectives and lax.ppermute only.
A program may use at most 64 MiB of HBM per device.

v0:
```python
import functools

import jax
import jax.numpy as jnp
from jax import lax
from jax.experimental import pallas as pl
from jax.experimental.pallas import tpu as pltpu
from jax.sharding import PartitionSpec as P

B = 32
W_BOND = 20
HALF = W_BOND // 2
PHYS = 4
SEC = 8
DAV_ITERS = 2
CAP = 2
N_SITE = 8
N_SECTOR = 32
SLOTS = N_SECTOR * CAP
ROWS = SEC * PHYS
LANES = SEC * B
PACK = 56
COUNT_ALL = float(N_SECTOR * SEC * B * B)
epsilon = 1e-06
bf16, f32 = jnp.bfloat16, jnp.float32
BOTH = ("site", "sector")


def flat(high, low_core, group, rest):
    return (high * 2 + low_core) * N_SECTOR + group * 8 + rest


def every_device():
    return [(y, c, g, r) for y in range(4) for c in range(2) for g in range(4) for r in range(8)]


def turn(block, step):
    pairs = [(flat(y, c, g, r), flat(g, c, (y + step) % 4, r)) for y, c, g, r in every_device()]
    return lax.ppermute(block, BOTH, pairs)


def exchange(block):
    groups = [
        [flat(y, c, g, r) for y in range(4) for r in range(8)] for g in range(4) for c in range(2)
    ]
    return lax.all_to_all(block, BOTH, split_axis=0, concat_axis=0, tiled=True, axis_index_groups=groups)


def other_core(block):
    return lax.ppermute(block, "site", [(i, i ^ 1) for i in range(N_SITE)])


def iota(shape, axis):
    return lax.broadcasted_iota(jnp.int32, shape, axis)


def block_mask(rows, lanes):
    same = (iota((rows, lanes), 0) // B) == (iota((rows, lanes), 1) // B)
    return jnp.where(same, 1.0, 0.0).astype(bf16)


def spread_blocks(field, mask):
    return jnp.concatenate([field] * SEC, axis=0) * mask


def column_block():
    return (iota((8, 128), 1) % B) // 8


def half_to_tiles(square):
    cb = column_block()

    def chosen(step, tile):
        parts = [tile[8 * d : 8 * d + 8, :] for d in range(4)]
        picked = parts[(3 + step) % 4]
        for d in (2, 1, 0):
            picked = jnp.where(cb == d, parts[(d + step) % 4], picked)
        return picked

    lane = iota((8, 128), 1)
    s = [[chosen(step, tile) for tile in square] for step in range(3)]
    return [
        s[0][0],
        s[0][1],
        s[1][0],
        s[1][1],
        jnp.where(lane < 64, s[0][2], pltpu.roll(s[1][2], 64, 1)),
        jnp.where(cb < 2, s[2][0], pltpu.roll(s[2][1], 16, 1)),
        s[2][2],
    ]


def tiles_to_half(tiles):
    cb = column_block()
    diag = [tiles[0], tiles[1], tiles[4]]
    near = [tiles[2], tiles[3], pltpu.roll(tiles[4], 64, 1)]
    far = [tiles[5], pltpu.roll(tiles[5], 112, 1), tiles[6]]
    square = []
    for tile in range(3):
        rows = []
        for d in range(4):
            rows.append(
                jnp.where(
                    cb == d, diag[tile], jnp.where(cb == (d - 1) % 4, near[tile], far[tile])
                )
            )
        square.append(jnp.concatenate(rows, axis=0))
    return square


def moved(sources, shifts):
    quarter = iota((B, 128), 1) // B
    total = None
    for k, (source, shift) in enumerate(zip(sources, shifts)):
        shift = shift % 128
        piece = pltpu.roll(source, shift, 1) if shift else source
        total = piece if total is None else jnp.where(quarter == k, piece, total)
    return total


def write_tall(core, mine_ref, other_ref, wide_ref, tall_ref):
    first = jnp.full((PACK, 128), core, jnp.int32) == 0
    ab = iota((B, LANES), 0) // 8
    bb = (iota((B, LANES), 1) % B) // 8
    gap = (ab - bb) & 3
    valid = (gap < 2) | ((gap == 2) & (bb < 2))
    for half in range(2):
        squares = []
        for t in range(SEC):
            mine, other = mine_ref[t].astype(f32), other_ref[t].astype(f32)
            whole = jnp.where(first, mine, other) if half == 0 else jnp.where(first, other, mine)
            square = tiles_to_half([whole[8 * i : 8 * i + 8, :] for i in range(7)])
            squares.append(square)
            for tile in range(3):
                wide_ref[t * B : (t + 1) * B, tile * 128 : (tile + 1) * 128] = square[tile]
        turned = jnp.transpose(wide_ref[...])
        bonds = []
        for v in range(HALF):
            tile, offset = v // 4, (v % 4) * B
            straight = jnp.concatenate(
                [
                    moved(
                        [squares[4 * q + k][tile] for k in range(4)],
                        [k * B - offset for k in range(4)],
                    )
                    for q in range(2)
                ],
                axis=1,
            )
            bonds.append(jnp.where(valid, straight, turned[v * B : (v + 1) * B, :]))
        for d in range(4):
            for v in range(0, HALF, 2):
                pair = [bonds[v + k][8 * d : 8 * d + 8, :] for k in range(2)]
                start = (d * W_BOND + half * HALF + v) * 8
                tall_ref[start : start + 16, :] = jnp.concatenate(pair, axis=0).astype(bf16)


def bond_rows(tall, bond, bonds=W_BOND):
    return jnp.concatenate(
        [tall[(d * bonds + bond) * 8 : (d * bonds + bond) * 8 + 8, :] for d in range(4)], axis=0
    )


def join_cores(core, near_ref, far_ref, tall_ref):
    first = jnp.full((HALF * B, LANES), core, jnp.int32) == 0
    near, far = near_ref[...].astype(f32), far_ref[...].astype(f32)
    low, high = jnp.where(first, near, far).astype(bf16), jnp.where(first, far, near).astype(bf16)
    step = HALF * 8
    for d in range(4):
        tall_ref[2 * d * step : (2 * d + 1) * step, :] = low[d * step : (d + 1) * step]
        tall_ref[(2 * d + 1) * step : (2 * d + 2) * step, :] = high[d * step : (d + 1) * step]


def contract_rows(i, info_ref, mpo_ref, tensor_ref, far_tensor_ref, tall, out_ref):
    place = info_ref[N_SITE, i]
    near_core = jnp.full((B, LANES), place, jnp.int32) < 4
    turned = place & 3
    mask = block_mask(LANES, LANES)
    mixer = mpo_ref[...]
    step = W_BOND * 8
    mixes = [
        jnp.dot(mixer, tall[d * step : (d + 1) * step, :], preferred_element_type=f32).astype(bf16)
        for d in range(4)
    ]
    for p in range(PHYS):
        mixed = jnp.concatenate(
            [mix[p * HALF * 8 : (p + 1) * HALF * 8, :] for mix in mixes], axis=0
        )
        rows = slice(p * B, (p + 1) * B)
        tensor = jnp.where(
            near_core, tensor_ref[turned, rows, :].astype(f32), far_tensor_ref[turned, rows, :].astype(f32)
        )
        right = spread_blocks(tensor.astype(bf16), mask)
        halfway = jnp.dot(mixed, right, preferred_element_type=f32)
        bonds = [bond_rows(halfway, v, HALF).astype(bf16) for v in range(HALF)]
        wide = []
        for s in range(SEC):
            source, offset = (s // 4) * 128, (s % 4) * B
            tiles = []
            for tile in range(3):
                here = [v for v in range(4 * tile, 4 * tile + 4) if v < HALF]
                tiles.append(
                    moved(
                        [bonds[v][:, source : source + 128] for v in here],
                        [(v % 4) * B - offset for v in here],
                    )
                )
            wide.append(jnp.concatenate(tiles, axis=1))
        wide = jnp.concatenate(wide, axis=0)
        blocks = lax.dot_general(right, wide, (((0,), (0,)), ((), ())), preferred_element_type=f32)
        for s in range(SEC):
            tiles = half_to_tiles(
                [blocks[s * B : (s + 1) * B, tile * 128 : (tile + 1) * 128] for tile in range(3)]
            )
            out_ref[info_ref[place, s * PHYS + p]] = jnp.concatenate(tiles, axis=0).astype(bf16)


def first_kernel(info_ref, mpo_ref, tensor_ref, far_tensor_ref, near_ref, far_ref, *rest):
    out_ref, tall_ref = rest
    join_cores(info_ref[N_SITE, N_SITE], near_ref, far_ref, tall_ref)
    contract_rows(0, info_ref, mpo_ref, tensor_ref, far_tensor_ref, tall_ref[...], out_ref)


def expand_kernel(i, info_ref, mpo_ref, tensor_ref, far_tensor_ref, mine_ref, other_ref, *rest):
    out_ref, tall_ref, wide_ref = rest
    write_tall(info_ref[N_SITE, N_SITE], mine_ref, other_ref, wide_ref, tall_ref)
    contract_rows(i, info_ref, mpo_ref, tensor_ref, far_tensor_ref, tall_ref[...], out_ref)


def collect_kernel(i, info_ref, inbox_ref, out_ref, total_ref):
    place = info_ref[N_SITE, i]
    total_ref[...] = jnp.zeros_like(total_ref)
    def take(turn_index, carry):
        for k in range(4):
            q = turn_index * 4 + k
            t = info_ref[place, ROWS + q]

            @pl.when(t > 0)
            def _():
                total_ref[t - 1] += inbox_ref[q].astype(f32)

        return carry

    lax.fori_loop(0, SLOTS // 4, take, 0)
    out_ref[...] = total_ref[...].astype(bf16)


VMEM = pl.BlockSpec(memory_space=pltpu.VMEM)
SMEM = pl.BlockSpec(memory_space=pltpu.SMEM)
PARAMS = pltpu.CompilerParams(vmem_limit_bytes=48 << 20)


def call(kernel, ins, outs, scratch=()):
    shapes = [jax.ShapeDtypeStruct(shape, dtype) for shape, dtype in outs]
    specs = [SMEM if x.dtype == jnp.int32 else VMEM for x in ins]
    return pl.pallas_call(
        kernel,
        out_shape=shapes,
        in_specs=specs,
        out_specs=[VMEM] * len(shapes),
        scratch_shapes=list(scratch),
        compiler_params=PARAMS,
        name=getattr(kernel, "func", kernel).__name__,
    )(*ins)


def run_expand(i, info, mpo, near, far, mine, other):
    (outbox,) = call(
        functools.partial(expand_kernel, i),
        [info, mpo, near, far, mine, other],
        [((SLOTS, PACK, 128), bf16)],
        [pltpu.VMEM((W_BOND * B, LANES), bf16), pltpu.VMEM((LANES, 384), f32)],
    )
    return outbox


def run_collect(i, info, inbox):
    (mine,) = call(
        functools.partial(collect_kernel, i),
        [info, inbox],
        [((SEC, PACK, 128), bf16)],
        [pltpu.VMEM((SEC, PACK, 128), f32)],
    )
    return mine


def apply_h(left, right_ref, field, mask):
    def parts(x):
        high = x.astype(bf16)
        return high, (x - high.astype(f32)).astype(bf16)

    high, low = parts(field)
    product = jnp.dot(left, spread_blocks(high, mask), preferred_element_type=f32)
    product = product + jnp.dot(left, spread_blocks(low, mask), preferred_element_type=f32)
    total = jnp.zeros((2 * B, LANES), f32)
    for w in range(W_BOND):
        rows = slice(w * B, (w + 1) * B)
        both = jnp.concatenate(parts(bond_rows(product, w)), axis=0)
        total = total + jnp.dot(
            both, spread_blocks(right_ref[rows, :], mask), preferred_element_type=f32
        )
    return total[:B] + total[B:]


def dot_all(former, latter):
    return jnp.sum(former * latter, axis=(0, 1), keepdims=True)


def send_sums(sums, sent_ref):
    lane = iota((1, 128), 1)
    row = jnp.zeros((1, 128), f32)
    for k, entry in enumerate(sums):
        row = jnp.where(lane == k, entry, row)
    sent_ref[...] = jnp.broadcast_to(row[None], (N_SECTOR, 1, 128))


def take_sums(got_ref, count):
    total = jnp.sum(got_ref[...], axis=0)
    return [total[:, k : k + 1] / COUNT_ALL for k in range(count)]


def live(extent_ref):
    extent = extent_ref[0:1, :].astype(jnp.int32)
    row, lane = iota((B, LANES), 0), iota((B, LANES), 1) % B
    return jnp.where((row < extent) & (lane < extent), 1.0, 0.0)


def start_kernel(last_ref, packed_ref, near_ref, far_ref, right_ref, psi_ref, extent_ref, *rest):
    left_ref, start_ref, image_ref, precond_ref, sent_ref, wide_ref = rest

    @pl.when(last_ref[0] > 0)
    def _():
        write_tall(last_ref[1], packed_ref.at[0], packed_ref.at[1], wide_ref, left_ref)

    @pl.when(last_ref[0] == 0)
    def _():
        join_cores(last_ref[1], near_ref, far_ref, left_ref)

    mask = block_mask(LANES, LANES)
    left = left_ref[...]
    alive = live(extent_ref)
    start = psi_ref[...].astype(f32) * alive
    image = apply_h(left, right_ref, start, mask) * alive
    diagonal = jnp.where(iota((B, LANES), 0) == iota((B, LANES), 1) % B, 1.0, 0.0)
    tall_row = iota((W_BOND * B, LANES), 0)
    tall_row = (tall_row // (W_BOND * 8)) * 8 + tall_row % 8
    on_diagonal = jnp.where(tall_row == iota((W_BOND * B, LANES), 1) % B, 1.0, 0.0)
    picked = on_diagonal.astype(bf16) * left
    left_diag = jnp.dot(picked, mask, preferred_element_type=f32)
    precond = jnp.zeros((B, LANES), f32)
    for w in range(W_BOND):
        rows = slice(w * B, (w + 1) * B)
        right_diag = jnp.sum(right_ref[rows, :].astype(f32) * diagonal, axis=0, keepdims=True)
        precond = precond + bond_rows(left_diag, w) * right_diag
    start_ref[...] = start
    image_ref[...] = image
    precond_ref[...] = precond
    send_sums([dot_all(start, start), dot_all(start, image)], sent_ref)


def next_correction(vector, image, energy, precond, left_ref, right_ref, alive, outs):
    vector_ref, image_ref, correction_ref, lifted_ref, sent_ref = outs
    residue = image - energy * vector
    correction = residue / jnp.maximum(precond - energy, 1.0)
    lifted = apply_h(left_ref[...], right_ref, correction, block_mask(LANES, LANES)) * alive
    vector_ref[...] = vector
    image_ref[...] = image
    correction_ref[...] = correction
    lifted_ref[...] = lifted
    send_sums(
        [
            dot_all(vector, correction),
            dot_all(correction, correction),
            dot_all(vector, vector),
            dot_all(correction, image),
            dot_all(correction, lifted),
            dot_all(vector, lifted),
            dot_all(vector, image),
        ],
        sent_ref,
    )


def one_kernel(got_ref, start_ref, raw_ref, precond_ref, left_ref, right_ref, extent_ref, *outs):
    norm, raw = take_sums(got_ref, 2)
    scale = 1.0 / jnp.sqrt(norm + epsilon)
    next_correction(
        start_ref[...] * scale,
        raw_ref[...] * scale,
        raw * scale * scale,
        precond_ref[...],
        left_ref,
        right_ref,
        live(extent_ref),
        outs,
    )


def rotated(got_ref, vector, image, correction, lifted):
    vc, cc, vv, ci, cl, vl, energy = take_sums(got_ref, 7)
    length_sq = jnp.maximum(cc - 2.0 * vc * vc + vc * vc * vv, 0.0)
    inverse = 1.0 / jnp.sqrt(length_sq + epsilon)
    direction = (correction - vc * vector) * inverse
    applied = (lifted - vc * image) * inverse
    coupling = (ci - vc * energy) * inverse
    crossed = (vl - vc * energy) * inverse
    curvature = (cl - vc * vl - vc * ci + vc * vc * energy) * inverse * inverse
    y, x = -2.0 * coupling, curvature - energy
    size = jnp.maximum(jnp.abs(x), jnp.abs(y))
    flat_case = size == 0.0
    size = jnp.where(flat_case, 1.0, size)
    y, x = y / size, jnp.where(flat_case, 1.0, x / size)
    radius = jnp.sqrt(x * x + y * y)
    large = jnp.sqrt((radius + jnp.abs(x)) / (2.0 * radius))
    small = jnp.abs(y) / (2.0 * radius * large)
    sign = jnp.where(y > 0.0, 1.0, -1.0)
    cosine = jnp.where(x >= 0.0, large, small)
    sine = sign * jnp.where(x >= 0.0, small, large)
    turned_energy = (
        cosine * cosine * energy + cosine * sine * (crossed + coupling) + sine * sine * curvature
    )
    return cosine * vector + sine * direction, cosine * image + sine * applied, turned_energy


def two_kernel(
    got_ref, v_ref, i_ref, c_ref, l_ref, precond_ref, left_ref, right_ref, extent_ref, *outs
):
    vector, image, energy = rotated(got_ref, v_ref[...], i_ref[...], c_ref[...], l_ref[...])
    next_correction(
        vector, image, energy, precond_ref[...], left_ref, right_ref, live(extent_ref), outs
    )


def last_kernel(got_ref, v_ref, i_ref, c_ref, l_ref, ground_ref):
    vector, image, energy = rotated(got_ref, v_ref[...], i_ref[...], c_ref[...], l_ref[...])
    ground_ref[0:B, :] = vector
    ground_ref[B : B + 8, :] = jnp.broadcast_to(energy, (8, LANES))


def slot_ranks(owner_grid):
    places = jnp.arange(owner_grid.shape[1])
    earlier = places[None, :] < places[:, None]
    same_owner = owner_grid[:, :, None] == owner_grid[:, None, :]
    return jnp.sum(jnp.where(same_owner & earlier[None], 1, 0), axis=2).astype(jnp.int32)


def tables(route_owner, route_sector, member):
    owner = route_owner.reshape(N_SECTOR, ROWS)
    worker = route_sector.reshape(N_SECTOR, ROWS)
    rank = slot_ranks(owner)
    slot = lax.dynamic_index_in_dim(owner * CAP + rank, member, 0, keepdims=False)
    mine = (owner == member)[:, None, :] & (rank[:, None, :] == jnp.arange(CAP)[None, :, None])
    target = jnp.sum(jnp.where(mine, worker[:, None, :] + 1, 0), axis=2)
    row = jnp.concatenate([slot, target.reshape(SLOTS)])
    return jnp.pad(row, (0, LANES - row.shape[0])).astype(bf16)


def local(
    env_in, mpo_terms, site_tensors, route_owner, route_sector, live_block_extent, psi, right_env
):
    site, sector = lax.axis_index("site"), lax.axis_index("sector")
    core, group = site % 2, sector // 8
    chain_site = group * 2 + core

    def tall(x):
        return x.reshape(SEC, W_BOND, B, B).transpose(1, 2, 0, 3).reshape(W_BOND * B, LANES)

    blocks = site_tensors.reshape(SEC, PHYS, B, B)
    table = tables(route_owner, route_sector, sector)
    tensors = jnp.concatenate(
        [
            blocks.transpose(1, 2, 0, 3).reshape(PHYS * B, LANES),
            jnp.broadcast_to(table[None], (8, LANES)),
        ],
        axis=0,
    )
    own_env = lax.dynamic_slice_in_dim(env_in, core * HALF, HALF, axis=1)
    own_env = own_env.reshape(SEC, HALF, 4, 8, B).transpose(2, 1, 3, 0, 4).reshape(HALF * B, LANES)
    near = jnp.stack([turn(tensors, step) for step in range(4)])
    near_env = turn(own_env, 0)
    far, far_env = other_core(near), other_core(near_env)
    sites = jnp.arange(N_SITE)
    places = jnp.where(sites % 2 == core, 0, 4) + (group - sites // 2) % 4
    places = jnp.pad(jnp.concatenate([places, core[None]]), (0, LANES - N_SITE - 1))
    info = jnp.concatenate([near[:, PHYS * B], far[:, PHYS * B]]).astype(jnp.int32)
    info = jnp.concatenate([info, places[None].astype(jnp.int32)])

    own_bonds = lax.dynamic_slice_in_dim(mpo_terms, core * HALF, HALF, axis=2)
    mpo = own_bonds.transpose(0, 2, 1).reshape(PHYS * HALF, 1, W_BOND, 1) * jnp.eye(8, dtype=bf16)[None, :, None, :]
    mpo = mpo.reshape(PHYS * HALF * 8, W_BOND * 8)

    davidson = jnp.concatenate(
        [
            tall(right_env),
            psi.reshape(SEC, B, B).transpose(1, 0, 2).reshape(B, LANES),
            jnp.broadcast_to(jnp.repeat(live_block_extent, B)[None], (8, LANES)).astype(bf16),
        ],
        axis=0,
    )

    outbox_shape = ((SLOTS, PACK, 128), bf16)
    tall_shape = ((W_BOND * B, LANES), bf16)
    wide_scratch = pltpu.VMEM((LANES, 384), f32)
    for i in range(N_SITE - 1):
        if i == 0:
            (outbox,) = call(first_kernel, [info, mpo, near, far, near_env, far_env], [outbox_shape], [pltpu.VMEM(*tall_shape)])
        else:
            outbox = run_expand(i, info, mpo, near, far, mine, other)
        mine = run_collect(i, info, exchange(outbox))
        other = other_core(mine)
        halves = jnp.stack([mine, other])
        saved = halves if i == 0 else jnp.where(chain_site == i + 1, halves, saved)
        if i == 0:
            mine, other, davidson = lax.optimization_barrier((mine, other, davidson))
            davidson = turn(davidson, 0)
        if i == 1:
            mine, other, davidson = lax.optimization_barrier((mine, other, davidson))

    right = davidson[: W_BOND * B]
    field, extent = davidson[W_BOND * B : W_BOND * B + B], davidson[W_BOND * B + B :]
    field_shape = ((B, LANES), f32)
    sums_shape = ((N_SECTOR, 1, 128), f32)
    last = jnp.stack([chain_site, core])
    left, start, raw, precond, sent = call(
        start_kernel,
        [last, saved, near_env, far_env, right, field, extent],
        [tall_shape, field_shape, field_shape, field_shape, sums_shape],
        [wide_scratch],
    )
    state = [start, raw]
    for step in range(DAV_ITERS):
        kernel = one_kernel if step == 0 else two_kernel
        *state, sent = call(
            kernel,
            [exchange(sent), *state, precond, left, right, extent],
            [field_shape] * 4 + [sums_shape],
        )
    (result,) = call(last_kernel, [exchange(sent), *state], [((B + 8, LANES), f32)])
    result = turn(result, 0)
    ground = result[:B].reshape(B, SEC, B).transpose(1, 0, 2).reshape(1, SEC, B * B)
    return (ground, result[B, :1])


def solution(mesh):
    in_specs = (
        P("sector", None, None),
        P(),
        P("site", "sector", None, None),
        P("site", None, None, None),
        P("site", None, None),
        P("sector"),
        P("site", "sector", None),
        P("site", "sector", None, None),
    )
    out_specs = (P("site", "sector", None), P("site"))
    return jax.shard_map(local, mesh=mesh, in_specs=in_specs, out_specs=out_specs, check_vma=False)
```

profile of v0, /device:TPU:16, one launch (start us, length us, event | category | flops | bytes accessed | tf_op | source)
XLA Modules:
  0.0 309.8 jit_solution(5833311675211575540)
XLA Ops:
  5.2 8.9 %collective-permute-start = (bf16[136,256]{1,0:T(8,128)(2,1)S(1)}, bf16[136,256]{1,0:T(8,128)(2,1)S(1)}, u32[]{:S(2)}, u32[]{:S(2)}) collective-permute-start(bf16[136,256]{1,0:T(8,128)(2,1)S(1)} %pad_maximum_fusion.2), channel_id=1, source_target_pairs={{0,0},{1,1},{2,2},{3,3},{4,4},{5,5},{6,6},{7,7},{8,64},{9,65},{10,... | collective-permute-start | bytes 208904 | tf_op jit(solution)/shard_map/ppermute | solution.py:39
  14.3 2.2 collective-permute-start.3
  17.7 8.3 %collective-permute-start.5 = (bf16[320,256]{1,0:T(8,128)(2,1)S(1)}, bf16[320,256]{1,0:T(8,128)(2,1)S(1)}, u32[]{:S(2)}, u32[]{:S(2)}) collective-permute-start(bf16[320,256]{1,0:T(8,128)(2,1)S(1)} %reshape.92), channel_id=1, source_target_pairs={{0,0},{1,1},{2,2},{3,3},{4,4},{5,5},{6,6},{7,7},{8,64},{9,65},{10,... | collective-permute-start | bytes 491528 | tf_op jit(solution)/shard_map/ppermute | solution.py:39
  29.0 2.9 collective-permute-done.5.near_ref
  33.2 3.5 %first_kernel.1 = bf16[64,56,128]{2,1,0:T(8,128)(2,1)} custom-call(s32[9,256]{1,0:T(8,128)S(1)} %pad_add_fusion.info_ref, bf16[320,160]{1,0:T(8,128)(2,1)S(1)} %copy.196.mpo_ref, bf16[4,136,256]{2,1,0:T(8,128)(2,1)S(1)} %copy.197.tensor_ref, bf16[4,136,256]{2,1,0:T(8,128)(2,1)S(1)} %copy.198.far_tensor_ref, ...), custom_call_target="tpu_custom_call" | custom-call | tf_op jit(solution)/shard_map/first_kernel/pallas_call | solution.py:256
  36.7 15.2 %all-to-all-start = ((bf16[64,56,128]{2,1,0:T(8,128)(2,1)}), bf16[64,56,128]{2,1,0:T(8,128)(2,1)S(1)}, u32[]{:S(2)}, u32[]{:S(2)}) async-start(bf16[64,56,128]{2,1,0:T(8,128)(2,1)} %first_kernel.1), calls=%async_computation | async-start | bytes 1835008 | tf_op jit(solution)/shard_map/all_to_all | solution.py:46
  51.9 2.1 reshape.93
  54.0 3.0 copy.204
  57.0 2.2 reshape.94
  59.6 5.8 %all-to-all-done.inbox_ref = bf16[64,56,128]{2,1,0:T(8,128)(2,1)S(1)} async-done(((bf16[64,56,128]{2,1,0:T(8,128)(2,1)}), bf16[64,56,128]{2,1,0:T(8,128)(2,1)S(1)}, u32[]{:S(2)}, u32[]{:S(2)}) %all-to-all-start) | async-done | bytes 917536 | tf_op jit(solution)/shard_map/all_to_all | solution.py:46
  68.5 3.9 %expand_kernel.6 = bf16[64,56,128]{2,1,0:T(8,128)(2,1)} custom-call(s32[9,256]{1,0:T(8,128)S(1)} %pad_add_fusion.info_ref, bf16[320,160]{1,0:T(8,128)(2,1)S(1)} %copy.196.mpo_ref, bf16[4,136,256]{2,1,0:T(8,128)(2,1)S(1)} %copy.197.tensor_ref, bf16[4,136,256]{2,1,0:T(8,128)(2,1)S(1)} %copy.198.far_tensor_ref, bf16[8,56,128]{2,1,0:T(8,128)(2,1)S(1)} %collect_kernel.7.mine_ref, ...), custom_call_target="tpu_custom_call" | custom-call | tf_op jit(solution)/shard_map/expand_kernel/pallas_call | solution.py:256
  72.4 7.2 %all-to-all-start.1 = ((bf16[64,56,128]{2,1,0:T(8,128)(2,1)}), bf16[64,56,128]{2,1,0:T(8,128)(2,1)S(1)}, u32[]{:S(2)}, u32[]{:S(2)}) async-start(bf16[64,56,128]{2,1,0:T(8,128)(2,1)} %expand_kernel.6), calls=%async_computation.1 | async-start | bytes 1835008 | tf_op jit(solution)/shard_map/all_to_all | solution.py:46
  79.6 1.9 collective-permute-start.9
  81.5 18.4 %all-to-all-done.1.inbox_ref = bf16[64,56,128]{2,1,0:T(8,128)(2,1)S(1)} async-done(((bf16[64,56,128]{2,1,0:T(8,128)(2,1)}), bf16[64,56,128]{2,1,0:T(8,128)(2,1)S(1)}, u32[]{:S(2)}, u32[]{:S(2)}) %all-to-all-start.1) | async-done | bytes 917536 | tf_op jit(solution)/shard_map/all_to_all | solution.py:46
  103.1 2.9 expand_kernel.7
  106.0 27.4 %all_to_all.50.inbox_ref = bf16[64,56,128]{2,1,0:T(8,128)(2,1)S(1)} all-to-all(bf16[64,56,128]{2,1,0:T(8,128)(2,1)S(1)} %expand_kernel.7), channel_id=1, replica_groups={{0,1,2,3,4,5,6,7,64,65,66,67,68,69,70,71,128,129,130,131,132,133,134,13..., dimensions={0} | all-to-all | bytes 1835008 | tf_op jit(solution)/shard_map/all_to_all | solution.py:46
  136.5 2.9 expand_kernel.8
  139.4 20.7 %all_to_all.51.inbox_ref = bf16[64,56,128]{2,1,0:T(8,128)(2,1)S(1)} all-to-all(bf16[64,56,128]{2,1,0:T(8,128)(2,1)S(1)} %expand_kernel.8), channel_id=1, replica_groups={{0,1,2,3,4,5,6,7,64,65,66,67,68,69,70,71,128,129,130,131,132,133,134,13..., dimensions={0} | all-to-all | bytes 1835008 | tf_op jit(solution)/shard_map/all_to_all | solution.py:46
  161.8 9.8 %collective-permute-start.11 = (bf16[8,56,128]{2,1,0:T(8,128)(2,1)S(1)}, bf16[8,56,128]{2,1,0:T(8,128)(2,1)S(1)}, u32[]{:S(2)}, u32[]{:S(2)}) collective-permute-start(bf16[8,56,128]{2,1,0:T(8,128)(2,1)S(1)} %collect_kernel.10.mine_ref), channel_id=1, source_target_pairs={{0,32},{32,0},{64,96},{96,64},{128,160},{160,128},{192,224},{224,1... | collective-permute-start | bytes 344072 | tf_op jit(solution)/shard_map/ppermute | solution.py:50
  173.0 2.9 expand_kernel.9
  175.9 20.6 %all_to_all.52.inbox_ref = bf16[64,56,128]{2,1,0:T(8,128)(2,1)S(1)} all-to-all(bf16[64,56,128]{2,1,0:T(8,128)(2,1)S(1)} %expand_kernel.9), channel_id=1, replica_groups={{0,1,2,3,4,5,6,7,64,65,66,67,68,69,70,71,128,129,130,131,132,133,134,13..., dimensions={0} | all-to-all | bytes 1835008 | tf_op jit(solution)/shard_map/all_to_all | solution.py:46
  199.6 2.9 expand_kernel.10
  202.6 20.6 %all_to_all.53.inbox_ref = bf16[64,56,128]{2,1,0:T(8,128)(2,1)S(1)} all-to-all(bf16[64,56,128]{2,1,0:T(8,128)(2,1)S(1)} %expand_kernel.10), channel_id=1, replica_groups={{0,1,2,3,4,5,6,7,64,65,66,67,68,69,70,71,128,129,130,131,132,133,134,13..., dimensions={0} | all-to-all | bytes 1835008 | tf_op jit(solution)/shard_map/all_to_all | solution.py:46
  226.3 2.9 expand_kernel.11
  229.3 20.6 %all_to_all.54.inbox_ref = bf16[64,56,128]{2,1,0:T(8,128)(2,1)S(1)} all-to-all(bf16[64,56,128]{2,1,0:T(8,128)(2,1)S(1)} %expand_kernel.11), channel_id=1, replica_groups={{0,1,2,3,4,5,6,7,64,65,66,67,68,69,70,71,128,129,130,131,132,133,134,13..., dimensions={0} | all-to-all | bytes 1835008 | tf_op jit(solution)/shard_map/all_to_all | solution.py:46
  253.1 2.0 start_kernel.1
  255.1 13.2 %all_to_all.55.got_ref = f32[32,1,128]{2,1,0:T(1,128)S(1)} all-to-all(f32[32,1,128]{2,1,0:T(1,128)S(1)} %get-tuple-element.29), channel_id=1, replica_groups={{0,1,2,3,4,5,6,7,64,65,66,67,68,69,70,71,128,129,130,131,132,133,134,13..., dimensions={0} | all-to-all | bytes 32768 | tf_op jit(solution)/shard_map/all_to_all | solution.py:46
  269.8 11.6 %all_to_all.56.got_ref = f32[32,1,128]{2,1,0:T(1,128)S(1)} all-to-all(f32[32,1,128]{2,1,0:T(1,128)S(1)} %get-tuple-element.34), channel_id=1, replica_groups={{0,1,2,3,4,5,6,7,64,65,66,67,68,69,70,71,128,129,130,131,132,133,134,13..., dimensions={0} | all-to-all | bytes 32768 | tf_op jit(solution)/shard_map/all_to_all | solution.py:46
  281.4 2.1 two_kernel.1
  283.6 11.6 %all_to_all.57.got_ref = f32[32,1,128]{2,1,0:T(1,128)S(1)} all-to-all(f32[32,1,128]{2,1,0:T(1,128)S(1)} %get-tuple-element.39), channel_id=1, replica_groups={{0,1,2,3,4,5,6,7,64,65,66,67,68,69,70,71,128,129,130,131,132,133,134,13..., dimensions={0} | all-to-all | bytes 32768 | tf_op jit(solution)/shard_map/all_to_all | solution.py:46
  296.1 4.2 %collective-permute-start.15 = (f32[40,256]{1,0:T(8,128)S(1)}, f32[40,256]{1,0:T(8,128)S(1)}, u32[]{:S(2)}, u32[]{:S(2)}) collective-permute-start(f32[40,256]{1,0:T(8,128)S(1)} %last_kernel.1), channel_id=1, source_target_pairs={{0,0},{1,1},{2,2},{3,3},{4,4},{5,5},{6,6},{7,7},{8,64},{9,65},{10,... | collective-permute-start | bytes 122888 | tf_op jit(solution)/shard_map/ppermute | solution.py:39
  300.3 8.0 %collective-permute-done.15 = f32[40,256]{1,0:T(8,128)S(1)} collective-permute-done((f32[40,256]{1,0:T(8,128)S(1)}, f32[40,256]{1,0:T(8,128)S(1)}, u32[]{:S(2)}, u32[]{:S(2)}) %collective-permute-start.15) | collective-permute-done | bytes 40992 | tf_op jit(solution)/shard_map/ppermute | solution.py:39
  (104 shorter events, 35.8 us)
Async XLA Ops:
  0.6 15.9 %copy-start = (bf16[8,20,1024]{2,0,1:T(8,128)(2,1)S(1)}, bf16[8,20,1024]{2,0,1:T(8,128)(2,1)}, u32[]{:S(2)}) copy-start(bf16[8,20,1024]{2,0,1:T(8,128)(2,1)} %param.8) | copy-start | bytes 983044
  5.2 21.2 %collective-permute-start = (bf16[136,256]{1,0:T(8,128)(2,1)S(1)}, bf16[136,256]{1,0:T(8,128)(2,1)S(1)}, u32[]{:S(2)}, u32[]{:S(2)}) collective-permute-start(bf16[136,256]{1,0:T(8,128)(2,1)S(1)} %pad_maximum_fusion.2), channel_id=1, source_target_pairs={{0,0},{1,1},{2,2},{3,3},{4,4},{5,5},{6,6},{7,7},{8,64},{9,65},{10,... | collective-permute-start | bytes 208904 | tf_op jit(solution)/shard_map/ppermute | solution.py:39
  14.1 12.4 %collective-permute-start.1 = (bf16[136,256]{1,0:T(8,128)(2,1)S(1)}, bf16[136,256]{1,0:T(8,128)(2,1)S(1)}, u32[]{:S(2)}, u32[]{:S(2)}) collective-permute-start(bf16[136,256]{1,0:T(8,128)(2,1)S(1)} %pad_maximum_fusion.2), channel_id=1, source_target_pairs={{0,8},{1,9},{2,10},{3,11},{4,12},{5,13},{6,14},{7,15},{8,72},{9,73... | collective-permute-start | bytes 208904 | tf_op jit(solution)/shard_map/ppermute | solution.py:39
  14.2 12.5 %collective-permute-start.2 = (bf16[136,256]{1,0:T(8,128)(2,1)S(1)}, bf16[136,256]{1,0:T(8,128)(2,1)S(1)}, u32[]{:S(2)}, u32[]{:S(2)}) collective-permute-start(bf16[136,256]{1,0:T(8,128)(2,1)S(1)} %pad_maximum_fusion.2), channel_id=1, source_target_pairs={{0,16},{1,17},{2,18},{3,19},{4,20},{5,21},{6,22},{7,23},{8,80},{9,... | collective-permute-start | bytes 208904 | tf_op jit(solution)/shard_map/ppermute | solution.py:39
  14.3 12.5 %collective-permute-start.3 = (bf16[136,256]{1,0:T(8,128)(2,1)S(1)}, bf16[136,256]{1,0:T(8,128)(2,1)S(1)}, u32[]{:S(2)}, u32[]{:S(2)}) collective-permute-start(bf16[136,256]{1,0:T(8,128)(2,1)S(1)} %pad_maximum_fusion.2), channel_id=1, source_target_pairs={{0,24},{1,25},{2,26},{3,27},{4,28},{5,29},{6,30},{7,31},{8,88},{9,... | collective-permute-start | bytes 208904 | tf_op jit(solution)/shard_map/ppermute | solution.py:39
  16.5 9.5 %copy-start.2 = (bf16[4,20,20]{2,0,1:T(4,128)(2,1)S(1)}, bf16[4,20,20]{2,0,1:T(4,128)(2,1)}, u32[]{:S(2)}) copy-start(bf16[4,20,20]{2,0,1:T(4,128)(2,1)} %param.9) | copy-start | bytes 9604
  17.7 14.1 %collective-permute-start.5 = (bf16[320,256]{1,0:T(8,128)(2,1)S(1)}, bf16[320,256]{1,0:T(8,128)(2,1)S(1)}, u32[]{:S(2)}, u32[]{:S(2)}) collective-permute-start(bf16[320,256]{1,0:T(8,128)(2,1)S(1)} %reshape.92), channel_id=1, source_target_pairs={{0,0},{1,1},{2,2},{3,3},{4,4},{5,5},{6,6},{7,7},{8,64},{9,65},{10,... | collective-permute-start | bytes 491528 | tf_op jit(solution)/shard_map/ppermute | solution.py:39
  27.6 4.3 %collective-permute-start.4 = (bf16[4,136,256]{2,0,1:T(4,128)(2,1)S(1)}, bf16[4,136,256]{2,0,1:T(4,128)(2,1)S(1)}, u32[]{:S(2)}, u32[]{:S(2)}) collective-permute-start(bf16[4,136,256]{2,0,1:T(4,128)(2,1)S(1)} %pad_maximum_fusion.1), channel_id=1, source_target_pairs={{0,32},{32,0},{64,96},{96,64},{128,160},{160,128},{192,224},{224,1... | collective-permute-start | bytes 835592 | tf_op jit(solution)/shard_map/ppermute | solution.py:50
  31.8 1.4 collective-permute-start.6
  31.9 20.0 %copy-start.1 = (bf16[1,8,20,1024]{3,1,2,0:T(8,128)(2,1)S(1)}, bf16[1,8,20,1024]{3,1,2,0:T(8,128)(2,1)}, u32[]{:S(2)}) copy-start(bf16[1,8,20,1024]{3,1,2,0:T(8,128)(2,1)} %param.15) | copy-start | bytes 983044
  36.7 28.7 %all-to-all-start = ((bf16[64,56,128]{2,1,0:T(8,128)(2,1)}), bf16[64,56,128]{2,1,0:T(8,128)(2,1)S(1)}, u32[]{:S(2)}, u32[]{:S(2)}) async-start(bf16[64,56,128]{2,1,0:T(8,128)(2,1)} %first_kernel.1), calls=%async_computation | async-start | bytes 1835008 | tf_op jit(solution)/shard_map/all_to_all | solution.py:46
  54.0 5.2 %copy-start.3 = (bf16[1,8,1024]{2,1,0:T(8,128)(2,1)S(1)}, bf16[1,8,1024]{2,1,0:T(8,128)(2,1)}, u32[]{:S(2)}) copy-start(bf16[1,8,1024]{2,1,0:T(8,128)(2,1)} %param.14) | copy-start | bytes 49156
  54.0 5.4 %copy-start.4 = (s32[8]{0:T(128)S(1)}, s32[8]{0:T(128)}, u32[]{:S(2)}) copy-start(s32[8]{0:T(128)} %param.13) | copy-start | bytes 100
  67.1 1.4 collective-permute-start.7
  72.4 27.5 %all-to-all-start.1 = ((bf16[64,56,128]{2,1,0:T(8,128)(2,1)}), bf16[64,56,128]{2,1,0:T(8,128)(2,1)S(1)}, u32[]{:S(2)}, u32[]{:S(2)}) async-start(bf16[64,56,128]{2,1,0:T(8,128)(2,1)} %expand_kernel.6), calls=%async_computation.1 | async-start | bytes 1835008 | tf_op jit(solution)/shard_map/all_to_all | solution.py:46
  79.6 22.7 %collective-permute-start.9 = (bf16[680,256]{1,0:T(8,128)(2,1)S(1)}, bf16[680,256]{1,0:T(8,128)(2,1)S(1)}, u32[]{:S(2)}, u32[]{:S(2)}) collective-permute-start(bf16[680,256]{1,0:T(8,128)(2,1)S(1)} %pad_maximum_fusion), channel_id=1, source_target_pairs={{0,0},{1,1},{2,2},{3,3},{4,4},{5,5},{6,6},{7,7},{8,64},{9,65},{10,... | collective-permute-start | bytes 1044488 | tf_op jit(solution)/shard_map/ppermute | solution.py:39
  101.7 1.4 collective-permute-start.8
  135.1 1.4 collective-permute-start.10
  161.8 11.2 %collective-permute-start.11 = (bf16[8,56,128]{2,1,0:T(8,128)(2,1)S(1)}, bf16[8,56,128]{2,1,0:T(8,128)(2,1)S(1)}, u32[]{:S(2)}, u32[]{:S(2)}) collective-permute-start(bf16[8,56,128]{2,1,0:T(8,128)(2,1)S(1)} %collect_kernel.10.mine_ref), channel_id=1, source_target_pairs={{0,32},{32,0},{64,96},{96,64},{128,160},{160,128},{192,224},{224,1... | collective-permute-start | bytes 344072 | tf_op jit(solution)/shard_map/ppermute | solution.py:50
  198.2 1.4 collective-permute-start.12
  224.9 1.4 collective-permute-start.13
  251.6 1.4 collective-permute-start.14
  296.1 12.2 %collective-permute-start.15 = (f32[40,256]{1,0:T(8,128)S(1)}, f32[40,256]{1,0:T(8,128)S(1)}, u32[]{:S(2)}, u32[]{:S(2)}) collective-permute-start(f32[40,256]{1,0:T(8,128)S(1)} %last_kernel.1), channel_id=1, source_target_pairs={{0,0},{1,1},{2,2},{3,3},{4,4},{5,5},{6,6},{7,7},{8,64},{9,65},{10,... | collective-permute-start | bytes 122888 | tf_op jit(solution)/shard_map/ppermute | solution.py:39
where the time goes:
time: 313 us; the launch traced here: 310 us
  blocking collectives  146 us (47%)
  starting transfers between devices  58.5 us (19%)
  waiting for transfers between devices  45.4 us (15%)
  Pallas kernels  40.5 us (13%)
  local copies, waits for them, and re-layouts  14.8 us (5%)
    all_to_all x8, blocking collectives, exchange(): lax.all_to_all(block, BOTH, split_axis=0, concat_axis=0, tiled=True, axis...  146 us
    pallas_call x18, Pallas kernels, call(): pl.pallas_call(kernel, out_shape=shapes, in_specs=specs, out_specs=[VMEM]...  40.5 us
    ppermute x7, starting transfers between devices, turn(): return lax.ppermute(block, BOTH, pairs)  25.6 us
    all_to_all x2, waiting for transfers between devices, exchange(): lax.all_to_all(block, BOTH, split_axis=0, concat_axis=0, tiled=True, axis...  24.2 us
    all_to_all x2, starting transfers between devices, exchange(): lax.all_to_all(block, BOTH, split_axis=0, concat_axis=0, tiled=True, axis...  22.3 us
    ppermute x7, waiting for transfers between devices, turn(): return lax.ppermute(block, BOTH, pairs)  11.4 us
    ppermute x9, starting transfers between devices, other_core(): return lax.ppermute(block, 'site', [(i, i ^ 1) for i in range(N_SITE)])  10.5 us
    ppermute x9, waiting for transfers between devices, other_core(): return lax.ppermute(block, 'site', [(i, i ^ 1) for i in range(N_SITE)])  9.75 us
  transfers between devices with their start and end apart: 18, of which 13 were waited for; matrix products, arithmetic and copies ran while one was open for 4% of the time, Pallas kernels for 1%

commit v1 on v0

--- a/solution.py
+++ b/solution.py
@@ -19,7 +19,7 @@
 SLOTS = N_SECTOR * CAP
 ROWS = SEC * PHYS
 LANES = SEC * B
-PACK = 56
+PACK = 48
 COUNT_ALL = float(N_SECTOR * SEC * B * B)
 epsilon = 1e-06
 bf16, f32 = jnp.bfloat16, jnp.float32
@@ -67,8 +67,35 @@
     return (iota((8, 128), 1) % B) // 8
 
 
-def half_to_tiles(square):
-    cb = column_block()
+def lane_map(sources):
+    return jnp.where(iota((128, 256), 0) == sources, 1.0, 0.0).astype(bf16)
+
+
+def outward():
+    lane = iota((128, 256), 1)
+    inner = lane % 128
+    source = ((inner // B) % 2) * B + 4 * ((inner % B) // 8) + inner % 4
+    used = (inner % 8 >= 4) & ((inner < 64) == (lane < 128))
+    return lane_map(jnp.where(used, source, -1))
+
+
+def inward():
+    lane = iota((128, 256), 1)
+    inner = lane % 128
+    source = (inner // B) * B + 8 * ((inner % B) // 4) + 4 + inner % 4
+    used = (inner < 64) & (inner % B < 16)
+    return lane_map(jnp.where(used, source + jnp.where(lane < 128, 0, 64), -1))
+
+
+def relocated(tiles, matrix):
+    stacked = jnp.concatenate(tiles, axis=0).astype(bf16)
+    images = jnp.dot(stacked, matrix, preferred_element_type=f32)
+    rows = [slice(8 * k, 8 * k + 8) for k in range(len(tiles))]
+    return [(images[r, :128], images[r, 128:]) for r in rows]
+
+
+def halves_to_tiles(squares, matrix):
+    cb, lane = column_block(), iota((8, 128), 1)
 
     def chosen(step, tile):
         parts = [tile[8 * d : 8 * d + 8, :] for d in range(4)]
@@ -77,24 +104,30 @@
             picked = jnp.where(cb == d, parts[(d + step) % 4], picked)
         return picked
 
-    lane = iota((8, 128), 1)
-    s = [[chosen(step, tile) for tile in square] for step in range(3)]
-    return [
-        s[0][0],
-        s[0][1],
-        s[1][0],
-        s[1][1],
-        jnp.where(lane < 64, s[0][2], pltpu.roll(s[1][2], 64, 1)),
-        jnp.where(cb < 2, s[2][0], pltpu.roll(s[2][1], 16, 1)),
-        s[2][2],
-    ]
-
-
-def tiles_to_half(tiles):
+    extras = relocated([chosen(2, square[2]) for square in squares], matrix)
+    for (first, second, third), (low, high) in zip(squares, extras):
+        near = pltpu.roll(chosen(1, third), 64, 1)
+        yield [
+            jnp.where(repeated(), low + pltpu.roll(high, 4, 0), chosen(0, first)),
+            chosen(0, second),
+            chosen(1, first),
+            chosen(1, second),
+            jnp.where(lane < 64, chosen(0, third), near),
+            jnp.where(cb < 2, chosen(2, first), pltpu.roll(chosen(2, second), 16, 1)),
+        ]
+
+
+def repeated():
+    return (iota((8, 128), 0) < 4) & (iota((8, 128), 1) % 8 >= 4)
+
+
+def tiles_to_half(tiles, extra):
     cb = column_block()
     diag = [tiles[0], tiles[1], tiles[4]]
     near = [tiles[2], tiles[3], pltpu.roll(tiles[4], 64, 1)]
-    far = [tiles[5], pltpu.roll(tiles[5], 112, 1), tiles[6]]
+    low, high = extra
+    extra = jnp.where(iota((8, 128), 0) < 4, low, pltpu.roll(high, 4, 0))
+    far = [tiles[5], pltpu.roll(tiles[5], 112, 1), extra]
     square = []
     for tile in range(3):
         rows = []
@@ -123,13 +156,20 @@
     ab = iota((B, LANES), 0) // 8
     bb = (iota((B, LANES), 1) % B) // 8
     gap = (ab - bb) & 3
-    valid = (gap < 2) | ((gap == 2) & (bb < 2))
+    spare = (gap == 0) & (iota((B, LANES), 0) % 8 < 4) & (iota((B, LANES), 1) % 8 >= 4)
+    matrix = inward()
+    valid = ((gap < 2) & jnp.logical_not(spare)) | ((gap == 2) & (bb < 2))
     for half in range(2):
+        def part(t, rows):
+            mine, other = mine_ref[t, rows, :].astype(f32), other_ref[t, rows, :].astype(f32)
+            here = first[rows]
+            return jnp.where(here, mine, other) if half == 0 else jnp.where(here, other, mine)
+
         squares = []
+        extras = relocated([part(t, slice(0, 16))[:8] for t in range(SEC)], matrix)
         for t in range(SEC):
-            mine, other = mine_ref[t].astype(f32), other_ref[t].astype(f32)
-            whole = jnp.where(first, mine, other) if half == 0 else jnp.where(first, other, mine)
-            square = tiles_to_half([whole[8 * i : 8 * i + 8, :] for i in range(7)])
+            whole = part(t, slice(0, PACK))
+            square = tiles_to_half([whole[8 * i : 8 * i + 8, :] for i in range(6)], extras[t])
             squares.append(square)
             for tile in range(3):
                 wide_ref[t * B : (t + 1) * B, tile * 128 : (tile + 1) * 128] = square[tile]
@@ -171,12 +211,12 @@
         tall_ref[(2 * d + 1) * step : (2 * d + 2) * step, :] = high[d * step : (d + 1) * step]
 
 
-def contract_rows(i, info_ref, mpo_ref, tensor_ref, far_tensor_ref, tall, out_ref):
-    place = info_ref[N_SITE, i]
+def contract_rows(step, info_ref, mpo_ref, tensor_ref, far_tensor_ref, tall, out_ref):
+    place = info_ref[N_SITE, step]
     near_core = jnp.full((B, LANES), place, jnp.int32) < 4
     turned = place & 3
     mask = block_mask(LANES, LANES)
-    mixer = mpo_ref[...]
+    mixer, matrix = mpo_ref[...], outward()
     step = W_BOND * 8
     mixes = [
         jnp.dot(mixer, tall[d * step : (d + 1) * step, :], preferred_element_type=f32).astype(bf16)
@@ -208,10 +248,11 @@
             wide.append(jnp.concatenate(tiles, axis=1))
         wide = jnp.concatenate(wide, axis=0)
         blocks = lax.dot_general(right, wide, (((0,), (0,)), ((), ())), preferred_element_type=f32)
-        for s in range(SEC):
-            tiles = half_to_tiles(
-                [blocks[s * B : (s + 1) * B, tile * 128 : (tile + 1) * 128] for tile in range(3)]
-            )
+        squares = [
+            [blocks[s * B : (s + 1) * B, tile * 128 : (tile + 1) * 128] for tile in range(3)]
+            for s in range(SEC)
+        ]
+        for s, tiles in enumerate(halves_to_tiles(squares, matrix)):
             out_ref[info_ref[place, s * PHYS + p]] = jnp.concatenate(tiles, axis=0).astype(bf16)
 
 
@@ -221,14 +262,14 @@
     contract_rows(0, info_ref, mpo_ref, tensor_ref, far_tensor_ref, tall_ref[...], out_ref)
 
 
-def expand_kernel(i, info_ref, mpo_ref, tensor_ref, far_tensor_ref, mine_ref, other_ref, *rest):
+def expand_kernel(step_ref, info_ref, mpo_ref, tensor_ref, far_tensor_ref, mine_ref, other_ref, *rest):
     out_ref, tall_ref, wide_ref = rest
     write_tall(info_ref[N_SITE, N_SITE], mine_ref, other_ref, wide_ref, tall_ref)
-    contract_rows(i, info_ref, mpo_ref, tensor_ref, far_tensor_ref, tall_ref[...], out_ref)
-
-
-def collect_kernel(i, info_ref, inbox_ref, out_ref, total_ref):
-    place = info_ref[N_SITE, i]
+    contract_rows(step_ref[0], info_ref, mpo_ref, tensor_ref, far_tensor_ref, tall_ref[...], out_ref)
+
+
+def collect_kernel(step_ref, info_ref, inbox_ref, out_ref, total_ref):
+    place = info_ref[N_SITE, step_ref[0]]
     total_ref[...] = jnp.zeros_like(total_ref)
     def take(turn_index, carry):
         for k in range(4):
@@ -266,8 +307,8 @@
 
 def run_expand(i, info, mpo, near, far, mine, other):
     (outbox,) = call(
-        functools.partial(expand_kernel, i),
-        [info, mpo, near, far, mine, other],
+        expand_kernel,
+        [i, info, mpo, near, far, mine, other],
         [((SLOTS, PACK, 128), bf16)],
         [pltpu.VMEM((W_BOND * B, LANES), bf16), pltpu.VMEM((LANES, 384), f32)],
     )
@@ -276,15 +317,15 @@
 
 def run_collect(i, info, inbox):
     (mine,) = call(
-        functools.partial(collect_kernel, i),
-        [info, inbox],
+        collect_kernel,
+        [i, info, inbox],
         [((SEC, PACK, 128), bf16)],
         [pltpu.VMEM((SEC, PACK, 128), f32)],
     )
     return mine
 
 
-def apply_h(left, right_ref, field, mask):
+def apply_h(left, right_ref, field, mask, product_ref):
     def parts(x):
         high = x.astype(bf16)
         return high, (x - high.astype(f32)).astype(bf16)
@@ -292,13 +333,20 @@
     high, low = parts(field)
     product = jnp.dot(left, spread_blocks(high, mask), preferred_element_type=f32)
     product = product + jnp.dot(left, spread_blocks(low, mask), preferred_element_type=f32)
-    total = jnp.zeros((2 * B, LANES), f32)
-    for w in range(W_BOND):
-        rows = slice(w * B, (w + 1) * B)
-        both = jnp.concatenate(parts(bond_rows(product, w)), axis=0)
-        total = total + jnp.dot(
-            both, spread_blocks(right_ref[rows, :], mask), preferred_element_type=f32
-        )
+    product_ref[...] = product
+
+    def one_group(group, total):
+        for k in range(5):
+            w = group * 5 + k
+            piece = jnp.concatenate(
+                [product_ref[pl.ds((d * W_BOND + w) * 8, 8), :] for d in range(4)], axis=0
+            )
+            both = jnp.concatenate(parts(piece), axis=0)
+            right = right_ref[pl.ds(pl.multiple_of(w * B, B), B), :]
+            total = total + jnp.dot(both, spread_blocks(right, mask), preferred_element_type=f32)
+        return total
+
+    total = lax.fori_loop(0, W_BOND // 5, one_group, jnp.zeros((2 * B, LANES), f32))
     return total[:B] + total[B:]
 
 
@@ -326,7 +374,7 @@
 
 
 def start_kernel(last_ref, packed_ref, near_ref, far_ref, right_ref, psi_ref, extent_ref, *rest):
-    left_ref, start_ref, image_ref, precond_ref, sent_ref, wide_ref = rest
+    left_ref, start_ref, image_ref, precond_ref, sent_ref, wide_ref, product_ref = rest
 
     @pl.when(last_ref[0] > 0)
     def _():
@@ -340,7 +388,7 @@
     left = left_ref[...]
     alive = live(extent_ref)
     start = psi_ref[...].astype(f32) * alive
-    image = apply_h(left, right_ref, start, mask) * alive
+    image = apply_h(left, right_ref, start, mask, product_ref) * alive
     diagonal = jnp.where(iota((B, LANES), 0) == iota((B, LANES), 1) % B, 1.0, 0.0)
     tall_row = iota((W_BOND * B, LANES), 0)
     tall_row = (tall_row // (W_BOND * 8)) * 8 + tall_row % 8
@@ -359,10 +407,10 @@
 
 
 def next_correction(vector, image, energy, precond, left_ref, right_ref, alive, outs):
-    vector_ref, image_ref, correction_ref, lifted_ref, sent_ref = outs
+    vector_ref, image_ref, correction_ref, lifted_ref, sent_ref, product_ref = outs
     residue = image - energy * vector
     correction = residue / jnp.maximum(precond - energy, 1.0)
-    lifted = apply_h(left_ref[...], right_ref, correction, block_mask(LANES, LANES)) * alive
+    lifted = apply_h(left_ref[...], right_ref, correction, block_mask(LANES, LANES), product_ref) * alive
     vector_ref[...] = vector
     image_ref[...] = image
     correction_ref[...] = correction
@@ -487,7 +535,7 @@
 
     own_bonds = lax.dynamic_slice_in_dim(mpo_terms, core * HALF, HALF, axis=2)
     mpo = own_bonds.transpose(0, 2, 1).reshape(PHYS * HALF, 1, W_BOND, 1) * jnp.eye(8, dtype=bf16)[None, :, None, :]
-    mpo = mpo.reshape(PHYS * HALF * 8, W_BOND * 8)
+    mpo = lax.optimization_barrier(mpo.reshape(PHYS * HALF * 8, W_BOND * 8))
 
     davidson = jnp.concatenate(
         [
@@ -501,20 +549,41 @@
     outbox_shape = ((SLOTS, PACK, 128), bf16)
     tall_shape = ((W_BOND * B, LANES), bf16)
     wide_scratch = pltpu.VMEM((LANES, 384), f32)
-    for i in range(N_SITE - 1):
-        if i == 0:
-            (outbox,) = call(first_kernel, [info, mpo, near, far, near_env, far_env], [outbox_shape], [pltpu.VMEM(*tall_shape)])
-        else:
-            outbox = run_expand(i, info, mpo, near, far, mine, other)
-        mine = run_collect(i, info, exchange(outbox))
+    product_scratch = pltpu.VMEM((W_BOND * B, LANES), f32)
+    def step_of(i):
+        return jnp.full((1,), i, jnp.int32)
+
+    def leave(i, outbox):
+        return run_collect(step_of(i), info, exchange(outbox))
+
+    def enter(i, mine, saved):
         other = other_core(mine)
-        halves = jnp.stack([mine, other])
-        saved = halves if i == 0 else jnp.where(chain_site == i + 1, halves, saved)
-        if i == 0:
-            mine, other, davidson = lax.optimization_barrier((mine, other, davidson))
-            davidson = turn(davidson, 0)
-        if i == 1:
-            mine, other, davidson = lax.optimization_barrier((mine, other, davidson))
+        return other, jnp.where(chain_site == i, jnp.stack([mine, other]), saved)
+
+    def one_site(i, mine, saved):
+        other, saved = enter(i, mine, saved)
+        return leave(i, run_expand(step_of(i), info, mpo, near, far, mine, other)), saved
+
+    (outbox,) = call(
+        first_kernel, [info, mpo, near, far, near_env, far_env], [outbox_shape], [pltpu.VMEM(*tall_shape)]
+    )
+    mine, saved = leave(0, outbox), jnp.zeros((2, SEC, PACK, 128), bf16)
+    other, saved = enter(1, mine, saved)
+    mine, other, davidson = lax.optimization_barrier((mine, other, davidson))
+    davidson = turn(davidson, 0)
+    mine = leave(1, run_expand(step_of(1), info, mpo, near, far, mine, other))
+    other, saved = enter(2, mine, saved)
+    mine, other, davidson, saved = lax.optimization_barrier((mine, other, davidson, saved))
+    mine = leave(2, run_expand(step_of(2), info, mpo, near, far, mine, other))
+
+    def two_sites(turn_index, state):
+        mine, saved = state
+        for k in range(2):
+            mine, saved = one_site(3 + 2 * turn_index + k, mine, saved)
+        return mine, saved
+
+    mine, saved = lax.fori_loop(0, 2, two_sites, (mine, saved))
+    other, saved = enter(N_SITE - 1, mine, saved)
 
     right = davidson[: W_BOND * B]
     field, extent = davidson[W_BOND * B : W_BOND * B + B], davidson[W_BOND * B + B :]
@@ -525,7 +594,7 @@
         start_kernel,
         [last, saved, near_env, far_env, right, field, extent],
         [tall_shape, field_shape, field_shape, field_shape, sums_shape],
-        [wide_scratch],
+        [wide_scratch, product_scratch],
     )
     state = [start, raw]
     for step in range(DAV_ITERS):
@@ -534,6 +603,7 @@
             kernel,
             [exchange(sent), *state, precond, left, right, extent],
             [field_shape] * 4 + [sums_shape],
+            [product_scratch],
         )
     (result,) = call(last_kernel, [exchange(sent), *state], [((B + 8, LANES), f32)])
     result = turn(result, 0)

time: 313 us -> 302 us (0.965)
  blocking collectives: 146 us -> 74 us
  waiting for transfers between devices: 45.4 us -> 81.2 us
  starting transfers between devices: 58.5 us -> 77.6 us
  Pallas kernels: 40.5 us -> 49 us
    all_to_all x8 -> x5, blocking collectives: 146 us -> 74 us  [exchange(): lax.all_to_all(block, BOTH, split_axis=0, concat_axis=0, tiled=True, axis...]
    all_to_all x2 -> x5, waiting for transfers between devices: 24.2 us -> 60.3 us  [exchange(): lax.all_to_all(block, BOTH, split_axis=0, concat_axis=0, tiled=True, axis...]
    all_to_all x2 -> x5, starting transfers between devices: 22.3 us -> 49.2 us  [exchange(): lax.all_to_all(block, BOTH, split_axis=0, concat_axis=0, tiled=True, axis...]
    ppermute x9, starting transfers between devices: 10.5 us -> 0.74 us  [other_core(): return lax.ppermute(block, 'site', [(i, i ^ 1) for i in range(N_SITE)])]
    pallas_call x18, Pallas kernels: 40.5 us -> 49 us  [call(): pl.pallas_call(kernel, out_shape=shapes, in_specs=specs, out_specs=[VMEM]...]
  transfers between devices with their start and end apart: 18 -> 21, of which waited for: 13 -> 15; matrix products, arithmetic and copies ran while one was open for 4% -> 4% of each run, Pallas kernels for 1% -> 1%
where the time goes in v1:
time: 302 us; the launch traced here: 301 us
  waiting for transfers between devices  81.2 us (27%)
  starting transfers between devices  77.6 us (26%)
  blocking collectives  74 us (25%)
  Pallas kernels  49 us (16%)
  local copies, waits for them, and re-layouts  14.8 us (5%)
    all_to_all x5, blocking collectives, exchange(): lax.all_to_all(block, BOTH, split_axis=0, concat_axis=0, tiled=True, axis...  74 us
    all_to_all x5, waiting for transfers between devices, exchange(): lax.all_to_all(block, BOTH, split_axis=0, concat_axis=0, tiled=True, axis...  60.3 us
    all_to_all x5, starting transfers between devices, exchange(): lax.all_to_all(block, BOTH, split_axis=0, concat_axis=0, tiled=True, axis...  49.2 us
    pallas_call x18, Pallas kernels, call(): pl.pallas_call(kernel, out_shape=shapes, in_specs=specs, out_specs=[VMEM]...  49 us
    ppermute x7, starting transfers between devices, turn(): return lax.ppermute(block, BOTH, pairs)  27.6 us
    ppermute x7, waiting for transfers between devices, turn(): return lax.ppermute(block, BOTH, pairs)  10.8 us
    ppermute x9, waiting for transfers between devices, other_core(): return lax.ppermute(block, 'site', [(i, i ^ 1) for i in range(N_SITE)])  10.1 us
    reshape x3, local copies, waits for them, and re-layouts, tall(): x.reshape(SEC, W_BOND, B, B).transpose(1, 2, 0, 3)  7.19 us
  transfers between devices with their start and end apart: 21, of which 15 were waited for; matrix products, arithmetic and copies ran while one was open for 4% of the time, Pallas kernels for 1%

profile of v1, /device:TPU:16, one launch (start us, length us, event | category | flops | bytes accessed | tf_op | source)
XLA Modules:
  0.0 300.9 jit_solution(13694426914557403627)
XLA Ops:
  5.3 3.1 %collective-permute-start.5 = (bf16[136,256]{1,0:T(8,128)(2,1)S(1)}, bf16[136,256]{1,0:T(8,128)(2,1)S(1)}, u32[]{:S(2)}, u32[]{:S(2)}) collective-permute-start(bf16[136,256]{1,0:T(8,128)(2,1)S(1)} %pad_maximum_fusion.2), channel_id=1, source_target_pairs={{0,24},{1,25},{2,26},{3,27},{4,28},{5,29},{6,30},{7,31},{8,88},{9,... | collective-permute-start | bytes 208904 | tf_op jit(solution)/shard_map/ppermute | solution.py:39
  8.4 3.6 %collective-permute-start.4 = (bf16[136,256]{1,0:T(8,128)(2,1)S(1)}, bf16[136,256]{1,0:T(8,128)(2,1)S(1)}, u32[]{:S(2)}, u32[]{:S(2)}) collective-permute-start(bf16[136,256]{1,0:T(8,128)(2,1)S(1)} %pad_maximum_fusion.2), channel_id=1, source_target_pairs={{0,16},{1,17},{2,18},{3,19},{4,20},{5,21},{6,22},{7,23},{8,80},{9,... | collective-permute-start | bytes 208904 | tf_op jit(solution)/shard_map/ppermute | solution.py:39
  12.0 4.1 %collective-permute-start.3 = (bf16[136,256]{1,0:T(8,128)(2,1)S(1)}, bf16[136,256]{1,0:T(8,128)(2,1)S(1)}, u32[]{:S(2)}, u32[]{:S(2)}) collective-permute-start(bf16[136,256]{1,0:T(8,128)(2,1)S(1)} %pad_maximum_fusion.2), channel_id=1, source_target_pairs={{0,8},{1,9},{2,10},{3,11},{4,12},{5,13},{6,14},{7,15},{8,72},{9,73... | collective-permute-start | bytes 208904 | tf_op jit(solution)/shard_map/ppermute | solution.py:39
  19.9 9.9 %collective-permute-start.7 = (bf16[320,256]{1,0:T(8,128)(2,1)S(1)}, bf16[320,256]{1,0:T(8,128)(2,1)S(1)}, u32[]{:S(2)}, u32[]{:S(2)}) collective-permute-start(bf16[320,256]{1,0:T(8,128)(2,1)S(1)} %reshape.92), channel_id=1, source_target_pairs={{0,0},{1,1},{2,2},{3,3},{4,4},{5,5},{6,6},{7,7},{8,64},{9,65},{10,... | collective-permute-start | bytes 491528 | tf_op jit(solution)/shard_map/ppermute | solution.py:39
  35.1 4.1 %first_kernel.1 = bf16[64,48,128]{2,1,0:T(8,128)(2,1)} custom-call(s32[9,256]{1,0:T(8,128)S(1)} %pad_add_fusion.info_ref, bf16[320,160]{1,0:T(8,128)(2,1)S(1)} %copy.142.mpo_ref, bf16[4,136,256]{2,1,0:T(8,128)(2,1)S(1)} %copy.143.tensor_ref, bf16[4,136,256]{2,1,0:T(8,128)(2,1)S(1)} %copy.144.far_tensor_ref, ...), custom_call_target="tpu_custom_call" | custom-call | tf_op jit(solution)/shard_map/first_kernel/pallas_call | solution.py:297
  39.2 14.9 %all-to-all-start.2 = ((bf16[64,48,128]{2,1,0:T(8,128)(2,1)}), bf16[64,48,128]{2,1,0:T(8,128)(2,1)S(1)}, u32[]{:S(2)}, u32[]{:S(2)}) async-start(bf16[64,48,128]{2,1,0:T(8,128)(2,1)} %first_kernel.1), calls=%async_computation.2 | async-start | bytes 1572864 | tf_op jit(solution)/shard_map/all_to_all | solution.py:46
  56.6 3.0 copy.153
  61.8 4.8 %all-to-all-done.2.inbox_ref = bf16[64,48,128]{2,1,0:T(8,128)(2,1)S(1)} async-done(((bf16[64,48,128]{2,1,0:T(8,128)(2,1)}), bf16[64,48,128]{2,1,0:T(8,128)(2,1)S(1)}, u32[]{:S(2)}, u32[]{:S(2)}) %all-to-all-start.2) | async-done | bytes 786464 | tf_op jit(solution)/shard_map/all_to_all | solution.py:46
  69.6 4.6 %expand_kernel.18 = bf16[64,48,128]{2,1,0:T(8,128)(2,1)} custom-call(s32[1]{0:T(128)} %constant.126.clone.1.step_ref, s32[9,256]{1,0:T(8,128)S(1)} %pad_add_fusion.info_ref, bf16[320,160]{1,0:T(8,128)(2,1)S(1)} %copy.142.mpo_ref, bf16[4,136,256]{2,1,0:T(8,128)(2,1)S(1)} %copy.143.tensor_ref, bf16[4,136,256]{2,1,0:T(8,128)(2,1)S(1)} %copy.144.far_tensor_ref, ...), custom_call_target="tpu_custom_call" | custom-call | tf_op jit(solution)/shard_map/expand_kernel/pallas_call | solution.py:297
  74.2 6.7 %all-to-all-start.3 = ((bf16[64,48,128]{2,1,0:T(8,128)(2,1)}), bf16[64,48,128]{2,1,0:T(8,128)(2,1)S(1)}, u32[]{:S(2)}, u32[]{:S(2)}) async-start(bf16[64,48,128]{2,1,0:T(8,128)(2,1)} %expand_kernel.18), calls=%async_computation.3 | async-start | bytes 1572864 | tf_op jit(solution)/shard_map/all_to_all | solution.py:46
  82.8 19.4 %all-to-all-done.3.inbox_ref = bf16[64,48,128]{2,1,0:T(8,128)(2,1)S(1)} async-done(((bf16[64,48,128]{2,1,0:T(8,128)(2,1)}), bf16[64,48,128]{2,1,0:T(8,128)(2,1)S(1)}, u32[]{:S(2)}, u32[]{:S(2)}) %all-to-all-start.3) | async-done | bytes 786464 | tf_op jit(solution)/shard_map/all_to_all | solution.py:46
  105.4 4.6 %expand_kernel.19 = bf16[64,48,128]{2,1,0:T(8,128)(2,1)} custom-call(s32[1]{0:T(128)} %constant.120.clone.1.step_ref, s32[9,256]{1,0:T(8,128)S(1)} %pad_add_fusion.info_ref, bf16[320,160]{1,0:T(8,128)(2,1)S(1)} %copy.142.mpo_ref, bf16[4,136,256]{2,1,0:T(8,128)(2,1)S(1)} %copy.143.tensor_ref, bf16[4,136,256]{2,1,0:T(8,128)(2,1)S(1)} %copy.144.far_tensor_ref, ...), custom_call_target="tpu_custom_call" | custom-call | tf_op jit(solution)/shard_map/expand_kernel/pallas_call | solution.py:297
  110.0 14.3 %all-to-all-start.4 = ((bf16[64,48,128]{2,1,0:T(8,128)(2,1)}), bf16[64,48,128]{2,1,0:T(8,128)(2,1)S(1)}, u32[]{:S(2)}, u32[]{:S(2)}) async-start(bf16[64,48,128]{2,1,0:T(8,128)(2,1)} %expand_kernel.19), calls=%async_computation.4 | async-start | bytes 1572864 | tf_op jit(solution)/shard_map/all_to_all | solution.py:46
  124.3 11.4 %all-to-all-done.4.inbox_ref = bf16[64,48,128]{2,1,0:T(8,128)(2,1)S(1)} async-done(((bf16[64,48,128]{2,1,0:T(8,128)(2,1)}), bf16[64,48,128]{2,1,0:T(8,128)(2,1)S(1)}, u32[]{:S(2)}, u32[]{:S(2)}) %all-to-all-start.4) | async-done | bytes 786464 | tf_op jit(solution)/shard_map/all_to_all | solution.py:46
  137.3 105.3 %while.17 = (s32[]{:T(128)}, bf16[8,48,128]{2,1,0:T(8,128)(2,1)S(1)}, bf16[2,8,48,128]{3,2,1,0:T(8,128)(2,1)S(1)}, s32[9,256]{1,0:T(8,128)S(1)}, bf16[320,160]{1...) while((s32[]{:T(128)}, ...), condition=%wide.region_3.4_spmd, body=%wide.region_2.3_spmd.sunk | while | flops 393223 | bytes 5505309 | solution.py:585
  138.7 3.7 %expand_kernel.20 = bf16[64,48,128]{2,1,0:T(8,128)(2,1)S(1)} custom-call(s32[1]{0:T(128)} %bitcast.68.step_ref, s32[9,256]{1,0:T(8,128)S(1)} %get-tuple-element.376.info_ref, bf16[320,160]{1,0:T(8,128)(2,1)S(1)} %get-tuple-element.377.mpo_ref, bf16[4,136,256]{2,1,0:T(8,128)(2,1)S(1)} %get-tuple-element.378.tensor_ref, ...), custom_call_target="tpu_custom_call" | custom-call | tf_op jit(solution)/shard_map/while/body/eval_jaxpr/expand_kernel/pallas_call | solution.py:297
  142.5 19.1 %all_to_all.45.inbox_ref = bf16[64,48,128]{2,1,0:T(8,128)(2,1)S(1)} all-to-all(bf16[64,48,128]{2,1,0:T(8,128)(2,1)S(1)} %expand_kernel.20), channel_id=1, replica_groups={{0,1,2,3,4,5,6,7,64,65,66,67,68,69,70,71,128,129,130,131,132,133,134,13..., dimensions={0} | all-to-all | bytes 1572864 | tf_op jit(solution)/shard_map/while/body/eval_jaxpr/all_to_all | solution.py:46
  164.6 4.6 %expand_kernel.21 = bf16[64,48,128]{2,1,0:T(8,128)(2,1)} custom-call(s32[1]{0:T(128)} %bitcast.67.step_ref, s32[9,256]{1,0:T(8,128)S(1)} %get-tuple-element.376.info_ref, bf16[320,160]{1,0:T(8,128)(2,1)S(1)} %get-tuple-element.377.mpo_ref, bf16[4,136,256]{2,1,0:T(8,128)(2,1)S(1)} %get-tuple-element.378.tensor_ref, ...), custom_call_target="tpu_custom_call" | custom-call | tf_op jit(solution)/shard_map/while/body/eval_jaxpr/expand_kernel/pallas_call | solution.py:297
  169.2 6.7 %all-to-all-start.1 = ((bf16[64,48,128]{2,1,0:T(8,128)(2,1)}), bf16[64,48,128]{2,1,0:T(8,128)(2,1)S(1)}, u32[]{:S(2)}, u32[]{:S(2)}) async-start(bf16[64,48,128]{2,1,0:T(8,128)(2,1)} %expand_kernel.21), calls=%async_computation.1 | async-start | bytes 1572864 | tf_op jit(solution)/shard_map/while/body/eval_jaxpr/all_to_all | solution.py:46
  176.0 12.4 %all-to-all-done.1.inbox_ref = bf16[64,48,128]{2,1,0:T(8,128)(2,1)S(1)} async-done(((bf16[64,48,128]{2,1,0:T(8,128)(2,1)}), bf16[64,48,128]{2,1,0:T(8,128)(2,1)S(1)}, u32[]{:S(2)}, u32[]{:S(2)}) %all-to-all-start.1) | async-done | bytes 786464 | tf_op jit(solution)/shard_map/while/body/eval_jaxpr/all_to_all | solution.py:46
  191.5 3.7 %expand_kernel.20 = bf16[64,48,128]{2,1,0:T(8,128)(2,1)S(1)} custom-call(s32[1]{0:T(128)} %bitcast.68.step_ref, s32[9,256]{1,0:T(8,128)S(1)} %get-tuple-element.376.info_ref, bf16[320,160]{1,0:T(8,128)(2,1)S(1)} %get-tuple-element.377.mpo_ref, bf16[4,136,256]{2,1,0:T(8,128)(2,1)S(1)} %get-tuple-element.378.tensor_ref, ...), custom_call_target="tpu_custom_call" | custom-call | tf_op jit(solution)/shard_map/while/body/eval_jaxpr/expand_kernel/pallas_call | solution.py:297
  195.2 18.9 %all_to_all.45.inbox_ref = bf16[64,48,128]{2,1,0:T(8,128)(2,1)S(1)} all-to-all(bf16[64,48,128]{2,1,0:T(8,128)(2,1)S(1)} %expand_kernel.20), channel_id=1, replica_groups={{0,1,2,3,4,5,6,7,64,65,66,67,68,69,70,71,128,129,130,131,132,133,134,13..., dimensions={0} | all-to-all | bytes 1572864 | tf_op jit(solution)/shard_map/while/body/eval_jaxpr/all_to_all | solution.py:46
  217.2 4.6 %expand_kernel.21 = bf16[64,48,128]{2,1,0:T(8,128)(2,1)} custom-call(s32[1]{0:T(128)} %bitcast.67.step_ref, s32[9,256]{1,0:T(8,128)S(1)} %get-tuple-element.376.info_ref, bf16[320,160]{1,0:T(8,128)(2,1)S(1)} %get-tuple-element.377.mpo_ref, bf16[4,136,256]{2,1,0:T(8,128)(2,1)S(1)} %get-tuple-element.378.tensor_ref, ...), custom_call_target="tpu_custom_call" | custom-call | tf_op jit(solution)/shard_map/while/body/eval_jaxpr/expand_kernel/pallas_call | solution.py:297
  221.8 6.7 %all-to-all-start.1 = ((bf16[64,48,128]{2,1,0:T(8,128)(2,1)}), bf16[64,48,128]{2,1,0:T(8,128)(2,1)S(1)}, u32[]{:S(2)}, u32[]{:S(2)}) async-start(bf16[64,48,128]{2,1,0:T(8,128)(2,1)} %expand_kernel.21), calls=%async_computation.1 | async-start | bytes 1572864 | tf_op jit(solution)/shard_map/while/body/eval_jaxpr/all_to_all | solution.py:46
  228.6 12.4 %all-to-all-done.1.inbox_ref = bf16[64,48,128]{2,1,0:T(8,128)(2,1)S(1)} async-done(((bf16[64,48,128]{2,1,0:T(8,128)(2,1)}), bf16[64,48,128]{2,1,0:T(8,128)(2,1)S(1)}, u32[]{:S(2)}, u32[]{:S(2)}) %all-to-all-start.1) | async-done | bytes 786464 | tf_op jit(solution)/shard_map/while/body/eval_jaxpr/all_to_all | solution.py:46
  244.1 2.3 start_kernel.1
  246.4 12.7 %all_to_all.42.got_ref = f32[32,1,128]{2,1,0:T(1,128)S(1)} all-to-all(f32[32,1,128]{2,1,0:T(1,128)S(1)} %get-tuple-element.221), channel_id=1, replica_groups={{0,1,2,3,4,5,6,7,64,65,66,67,68,69,70,71,128,129,130,131,132,133,134,13..., dimensions={0} | all-to-all | bytes 32768 | tf_op jit(solution)/shard_map/all_to_all | solution.py:46
  260.9 11.6 %all_to_all.43.got_ref = f32[32,1,128]{2,1,0:T(1,128)S(1)} all-to-all(f32[32,1,128]{2,1,0:T(1,128)S(1)} %get-tuple-element.226), channel_id=1, replica_groups={{0,1,2,3,4,5,6,7,64,65,66,67,68,69,70,71,128,129,130,131,132,133,134,13..., dimensions={0} | all-to-all | bytes 32768 | tf_op jit(solution)/shard_map/all_to_all | solution.py:46
  272.5 2.4 two_kernel.1
  274.9 11.6 %all_to_all.44.got_ref = f32[32,1,128]{2,1,0:T(1,128)S(1)} all-to-all(f32[32,1,128]{2,1,0:T(1,128)S(1)} %get-tuple-element.231), channel_id=1, replica_groups={{0,1,2,3,4,5,6,7,64,65,66,67,68,69,70,71,128,129,130,131,132,133,134,13..., dimensions={0} | all-to-all | bytes 32768 | tf_op jit(solution)/shard_map/all_to_all | solution.py:46
  287.4 2.8 collective-permute-start.13
  290.2 9.4 %collective-permute-done.13 = f32[40,256]{1,0:T(8,128)S(1)} collective-permute-done((f32[40,256]{1,0:T(8,128)S(1)}, f32[40,256]{1,0:T(8,128)S(1)}, u32[]{:S(2)}, u32[]{:S(2)}) %collective-permute-start.13) | collective-permute-done | bytes 40992 | tf_op jit(solution)/shard_map/ppermute | solution.py:39
  (111 shorter events, 45.4 us)
Async XLA Ops:
  0.6 17.9 %copy-start = (bf16[8,20,1024]{2,0,1:T(8,128)(2,1)S(1)}, bf16[8,20,1024]{2,0,1:T(8,128)(2,1)}, u32[]{:S(2)}) copy-start(bf16[8,20,1024]{2,0,1:T(8,128)(2,1)} %param.10) | copy-start | bytes 983044
  0.6 17.7 %copy-start.2 = (bf16[4,20,20]{2,0,1:T(4,128)(2,1)S(1)}, bf16[4,20,20]{2,0,1:T(4,128)(2,1)}, u32[]{:S(2)}) copy-start(bf16[4,20,20]{2,0,1:T(4,128)(2,1)} %param.11) | copy-start | bytes 9604
  5.3 24.6 %collective-permute-start.5 = (bf16[136,256]{1,0:T(8,128)(2,1)S(1)}, bf16[136,256]{1,0:T(8,128)(2,1)S(1)}, u32[]{:S(2)}, u32[]{:S(2)}) collective-permute-start(bf16[136,256]{1,0:T(8,128)(2,1)S(1)} %pad_maximum_fusion.2), channel_id=1, source_target_pairs={{0,24},{1,25},{2,26},{3,27},{4,28},{5,29},{6,30},{7,31},{8,88},{9,... | collective-permute-start | bytes 208904 | tf_op jit(solution)/shard_map/ppermute | solution.py:39
  8.4 21.6 %collective-permute-start.4 = (bf16[136,256]{1,0:T(8,128)(2,1)S(1)}, bf16[136,256]{1,0:T(8,128)(2,1)S(1)}, u32[]{:S(2)}, u32[]{:S(2)}) collective-permute-start(bf16[136,256]{1,0:T(8,128)(2,1)S(1)} %pad_maximum_fusion.2), channel_id=1, source_target_pairs={{0,16},{1,17},{2,18},{3,19},{4,20},{5,21},{6,22},{7,23},{8,80},{9,... | collective-permute-start | bytes 208904 | tf_op jit(solution)/shard_map/ppermute | solution.py:39
  12.0 18.1 %collective-permute-start.3 = (bf16[136,256]{1,0:T(8,128)(2,1)S(1)}, bf16[136,256]{1,0:T(8,128)(2,1)S(1)}, u32[]{:S(2)}, u32[]{:S(2)}) collective-permute-start(bf16[136,256]{1,0:T(8,128)(2,1)S(1)} %pad_maximum_fusion.2), channel_id=1, source_target_pairs={{0,8},{1,9},{2,10},{3,11},{4,12},{5,13},{6,14},{7,15},{8,72},{9,73... | collective-permute-start | bytes 208904 | tf_op jit(solution)/shard_map/ppermute | solution.py:39
  16.1 14.2 %collective-permute-start.2 = (bf16[136,256]{1,0:T(8,128)(2,1)S(1)}, bf16[136,256]{1,0:T(8,128)(2,1)S(1)}, u32[]{:S(2)}, u32[]{:S(2)}) collective-permute-start(bf16[136,256]{1,0:T(8,128)(2,1)S(1)} %pad_maximum_fusion.2), channel_id=1, source_target_pairs={{0,0},{1,1},{2,2},{3,3},{4,4},{5,5},{6,6},{7,7},{8,64},{9,65},{10,... | collective-permute-start | bytes 208904 | tf_op jit(solution)/shard_map/ppermute | solution.py:39
  19.9 13.8 %collective-permute-start.7 = (bf16[320,256]{1,0:T(8,128)(2,1)S(1)}, bf16[320,256]{1,0:T(8,128)(2,1)S(1)}, u32[]{:S(2)}, u32[]{:S(2)}) collective-permute-start(bf16[320,256]{1,0:T(8,128)(2,1)S(1)} %reshape.92), channel_id=1, source_target_pairs={{0,0},{1,1},{2,2},{3,3},{4,4},{5,5},{6,6},{7,7},{8,64},{9,65},{10,... | collective-permute-start | bytes 491528 | tf_op jit(solution)/shard_map/ppermute | solution.py:39
  31.0 2.7 collective-permute-start.6
  33.7 1.4 collective-permute-start.8
  33.8 20.3 %copy-start.4 = (s32[8]{0:T(128)S(1)}, s32[8]{0:T(128)}, u32[]{:S(2)}) copy-start(s32[8]{0:T(128)} %param.15) | copy-start | bytes 100
  33.8 20.5 %copy-start.3 = (bf16[1,8,1024]{2,1,0:T(8,128)(2,1)S(1)}, bf16[1,8,1024]{2,1,0:T(8,128)(2,1)}, u32[]{:S(2)}) copy-start(bf16[1,8,1024]{2,1,0:T(8,128)(2,1)} %param.16) | copy-start | bytes 49156
  33.8 20.7 %copy-start.1 = (bf16[1,8,20,1024]{3,1,2,0:T(8,128)(2,1)S(1)}, bf16[1,8,20,1024]{3,1,2,0:T(8,128)(2,1)}, u32[]{:S(2)}) copy-start(bf16[1,8,20,1024]{3,1,2,0:T(8,128)(2,1)} %param.17) | copy-start | bytes 983044
  39.2 27.3 %all-to-all-start.2 = ((bf16[64,48,128]{2,1,0:T(8,128)(2,1)}), bf16[64,48,128]{2,1,0:T(8,128)(2,1)S(1)}, u32[]{:S(2)}, u32[]{:S(2)}) async-start(bf16[64,48,128]{2,1,0:T(8,128)(2,1)} %first_kernel.1), calls=%async_computation.2 | async-start | bytes 1572864 | tf_op jit(solution)/shard_map/all_to_all | solution.py:46
  68.2 1.4 collective-permute-start.9
  74.2 28.0 %all-to-all-start.3 = ((bf16[64,48,128]{2,1,0:T(8,128)(2,1)}), bf16[64,48,128]{2,1,0:T(8,128)(2,1)S(1)}, u32[]{:S(2)}, u32[]{:S(2)}) async-start(bf16[64,48,128]{2,1,0:T(8,128)(2,1)} %expand_kernel.18), calls=%async_computation.3 | async-start | bytes 1572864 | tf_op jit(solution)/shard_map/all_to_all | solution.py:46
  80.9 24.5 %collective-permute-start.11 = (bf16[680,256]{1,0:T(8,128)(2,1)S(1)}, bf16[680,256]{1,0:T(8,128)(2,1)S(1)}, u32[]{:S(2)}, u32[]{:S(2)}) collective-permute-start(bf16[680,256]{1,0:T(8,128)(2,1)S(1)} %pad_maximum_fusion), channel_id=1, source_target_pairs={{0,0},{1,1},{2,2},{3,3},{4,4},{5,5},{6,6},{7,7},{8,64},{9,65},{10,... | collective-permute-start | bytes 1044488 | tf_op jit(solution)/shard_map/ppermute | solution.py:39
  103.9 1.4 collective-permute-start.10
  110.0 25.7 %all-to-all-start.4 = ((bf16[64,48,128]{2,1,0:T(8,128)(2,1)}), bf16[64,48,128]{2,1,0:T(8,128)(2,1)S(1)}, u32[]{:S(2)}, u32[]{:S(2)}) async-start(bf16[64,48,128]{2,1,0:T(8,128)(2,1)} %expand_kernel.19), calls=%async_computation.4 | async-start | bytes 1572864 | tf_op jit(solution)/shard_map/all_to_all | solution.py:46
  137.4 1.4 collective-permute-start
  163.2 1.4 collective-permute-start.1
  169.2 19.2 %all-to-all-start.1 = ((bf16[64,48,128]{2,1,0:T(8,128)(2,1)}), bf16[64,48,128]{2,1,0:T(8,128)(2,1)S(1)}, u32[]{:S(2)}, u32[]{:S(2)}) async-start(bf16[64,48,128]{2,1,0:T(8,128)(2,1)} %expand_kernel.21), calls=%async_computation.1 | async-start | bytes 1572864 | tf_op jit(solution)/shard_map/while/body/eval_jaxpr/all_to_all | solution.py:46
  190.1 1.4 collective-permute-start
  215.8 1.4 collective-permute-start.1
  221.8 19.2 %all-to-all-start.1 = ((bf16[64,48,128]{2,1,0:T(8,128)(2,1)}), bf16[64,48,128]{2,1,0:T(8,128)(2,1)S(1)}, u32[]{:S(2)}, u32[]{:S(2)}) async-start(bf16[64,48,128]{2,1,0:T(8,128)(2,1)} %expand_kernel.21), calls=%async_computation.1 | async-start | bytes 1572864 | tf_op jit(solution)/shard_map/while/body/eval_jaxpr/all_to_all | solution.py:46
  242.7 1.4 collective-permute-start.12
  287.4 12.2 %collective-permute-start.13 = (f32[40,256]{1,0:T(8,128)S(1)}, f32[40,256]{1,0:T(8,128)S(1)}, u32[]{:S(2)}, u32[]{:S(2)}) collective-permute-start(f32[40,256]{1,0:T(8,128)S(1)} %last_kernel.1), channel_id=1, source_target_pairs={{0,0},{1,1},{2,2},{3,3},{4,4},{5,5},{6,6},{7,7},{8,64},{9,65},{10,... | collective-permute-start | bytes 122888 | tf_op jit(solution)/shard_map/ppermute | solution.py:39

commit v2 on v1

--- a/solution.py
+++ b/solution.py
@@ -573,7 +573,10 @@
     davidson = turn(davidson, 0)
     mine = leave(1, run_expand(step_of(1), info, mpo, near, far, mine, other))
     other, saved = enter(2, mine, saved)
-    mine, other, davidson, saved = lax.optimization_barrier((mine, other, davidson, saved))
+    closing = chain_site == N_SITE - 1
+    mine, other, davidson, saved, closing = lax.optimization_barrier(
+        (mine, other, davidson, saved, closing)
+    )
     mine = leave(2, run_expand(step_of(2), info, mpo, near, far, mine, other))
 
     def two_sites(turn_index, state):
@@ -583,7 +586,8 @@
         return mine, saved
 
     mine, saved = lax.fori_loop(0, 2, two_sites, (mine, saved))
-    other, saved = enter(N_SITE - 1, mine, saved)
+    other = other_core(mine)
+    saved = jnp.where(closing, jnp.stack([mine, other]), saved)
 
     right = davidson[: W_BOND * B]
     field, extent = davidson[W_BOND * B : W_BOND * B + B], davidson[W_BOND * B + B :]

time: 302 us -> 301 us (level)
  blocking collectives: 74 us -> 99.1 us
  starting transfers between devices: 77.6 us -> 63.1 us
  waiting for transfers between devices: 81.2 us -> 69.9 us
    all_to_all x5 -> x6, blocking collectives: 74 us -> 99.1 us  [exchange(): lax.all_to_all(block, BOTH, split_axis=0, concat_axis=0, tiled=True, axis...]
    all_to_all x5 -> x4, starting transfers between devices: 49.2 us -> 34.8 us  [exchange(): lax.all_to_all(block, BOTH, split_axis=0, concat_axis=0, tiled=True, axis...]
    all_to_all x5 -> x4, waiting for transfers between devices: 60.3 us -> 49 us  [exchange(): lax.all_to_all(block, BOTH, split_axis=0, concat_axis=0, tiled=True, axis...]
  transfers between devices with their start and end apart: 21 -> 20, of which waited for: 15 -> 14; matrix products, arithmetic and copies ran while one was open for 4% -> 4% of each run, Pallas kernels for 1% -> 1%
where the time goes in v2:
time: 301 us; the launch traced here: 300 us
  blocking collectives  99.1 us (33%)
  waiting for transfers between devices  69.9 us (23%)
  starting transfers between devices  63.1 us (21%)
  Pallas kernels  48.6 us (16%)
  local copies, waits for them, and re-layouts  14.8 us (5%)
    all_to_all x6, blocking collectives, exchange(): lax.all_to_all(block, BOTH, split_axis=0, concat_axis=0, tiled=True, axis...  99.1 us
    all_to_all x4, waiting for transfers between devices, exchange(): lax.all_to_all(block, BOTH, split_axis=0, concat_axis=0, tiled=True, axis...  49 us
    pallas_call x18, Pallas kernels, call(): pl.pallas_call(kernel, out_shape=shapes, in_specs=specs, out_specs=[VMEM]...  48.6 us
    all_to_all x4, starting transfers between devices, exchange(): lax.all_to_all(block, BOTH, split_axis=0, concat_axis=0, tiled=True, axis...  34.8 us
    ppermute x7, starting transfers between devices, turn(): return lax.ppermute(block, BOTH, pairs)  27.6 us
    ppermute x7, waiting for transfers between devices, turn(): return lax.ppermute(block, BOTH, pairs)  10.8 us
    ppermute x9, waiting for transfers between devices, other_core(): return lax.ppermute(block, 'site', [(i, i ^ 1) for i in range(N_SITE)])  10.1 us
    reshape x3, local copies, waits for them, and re-layouts, tall(): x.reshape(SEC, W_BOND, B, B).transpose(1, 2, 0, 3)  7.18 us
  transfers between devices with their start and end apart: 20, of which 14 were waited for; matrix products, arithmetic and copies ran while one was open for 4% of the time, Pallas kernels for 1%

profile of v2, /device:TPU:16, one launch (start us, length us, event | category | flops | bytes accessed | tf_op | source)
XLA Modules:
  0.0 299.9 jit_solution(6717687773999803204)
XLA Ops:
  5.3 3.1 %collective-permute-start.5 = (bf16[136,256]{1,0:T(8,128)(2,1)S(1)}, bf16[136,256]{1,0:T(8,128)(2,1)S(1)}, u32[]{:S(2)}, u32[]{:S(2)}) collective-permute-start(bf16[136,256]{1,0:T(8,128)(2,1)S(1)} %pad_maximum_fusion.2), channel_id=1, source_target_pairs={{0,24},{1,25},{2,26},{3,27},{4,28},{5,29},{6,30},{7,31},{8,88},{9,... | collective-permute-start | bytes 208904 | tf_op jit(solution)/shard_map/ppermute | solution.py:39
  8.4 3.6 %collective-permute-start.4 = (bf16[136,256]{1,0:T(8,128)(2,1)S(1)}, bf16[136,256]{1,0:T(8,128)(2,1)S(1)}, u32[]{:S(2)}, u32[]{:S(2)}) collective-permute-start(bf16[136,256]{1,0:T(8,128)(2,1)S(1)} %pad_maximum_fusion.2), channel_id=1, source_target_pairs={{0,16},{1,17},{2,18},{3,19},{4,20},{5,21},{6,22},{7,23},{8,80},{9,... | collective-permute-start | bytes 208904 | tf_op jit(solution)/shard_map/ppermute | solution.py:39
  12.0 4.1 %collective-permute-start.3 = (bf16[136,256]{1,0:T(8,128)(2,1)S(1)}, bf16[136,256]{1,0:T(8,128)(2,1)S(1)}, u32[]{:S(2)}, u32[]{:S(2)}) collective-permute-start(bf16[136,256]{1,0:T(8,128)(2,1)S(1)} %pad_maximum_fusion.2), channel_id=1, source_target_pairs={{0,8},{1,9},{2,10},{3,11},{4,12},{5,13},{6,14},{7,15},{8,72},{9,73... | collective-permute-start | bytes 208904 | tf_op jit(solution)/shard_map/ppermute | solution.py:39
  16.1 2.2 collective-permute-start.2
  19.9 9.9 %collective-permute-start.7 = (bf16[320,256]{1,0:T(8,128)(2,1)S(1)}, bf16[320,256]{1,0:T(8,128)(2,1)S(1)}, u32[]{:S(2)}, u32[]{:S(2)}) collective-permute-start(bf16[320,256]{1,0:T(8,128)(2,1)S(1)} %reshape.92), channel_id=1, source_target_pairs={{0,0},{1,1},{2,2},{3,3},{4,4},{5,5},{6,6},{7,7},{8,64},{9,65},{10,... | collective-permute-start | bytes 491528 | tf_op jit(solution)/shard_map/ppermute | solution.py:39
  35.1 4.1 %first_kernel.1 = bf16[64,48,128]{2,1,0:T(8,128)(2,1)} custom-call(s32[9,256]{1,0:T(8,128)S(1)} %pad_add_fusion.info_ref, bf16[320,160]{1,0:T(8,128)(2,1)S(1)} %copy.139.mpo_ref, bf16[4,136,256]{2,1,0:T(8,128)(2,1)S(1)} %copy.140.tensor_ref, bf16[4,136,256]{2,1,0:T(8,128)(2,1)S(1)} %copy.141.far_tensor_ref, ...), custom_call_target="tpu_custom_call" | custom-call | tf_op jit(solution)/shard_map/first_kernel/pallas_call | solution.py:297
  39.2 14.9 %all-to-all-start.2 = ((bf16[64,48,128]{2,1,0:T(8,128)(2,1)}), bf16[64,48,128]{2,1,0:T(8,128)(2,1)S(1)}, u32[]{:S(2)}, u32[]{:S(2)}) async-start(bf16[64,48,128]{2,1,0:T(8,128)(2,1)} %first_kernel.1), calls=%async_computation.2 | async-start | bytes 1572864 | tf_op jit(solution)/shard_map/all_to_all | solution.py:46
  56.6 2.9 copy.153
  61.7 4.8 %all-to-all-done.2.inbox_ref = bf16[64,48,128]{2,1,0:T(8,128)(2,1)S(1)} async-done(((bf16[64,48,128]{2,1,0:T(8,128)(2,1)}), bf16[64,48,128]{2,1,0:T(8,128)(2,1)S(1)}, u32[]{:S(2)}, u32[]{:S(2)}) %all-to-all-start.2) | async-done | bytes 786464 | tf_op jit(solution)/shard_map/all_to_all | solution.py:46
  69.7 4.6 %expand_kernel.18 = bf16[64,48,128]{2,1,0:T(8,128)(2,1)} custom-call(s32[1]{0:T(128)} %constant.120.clone.1.step_ref, s32[9,256]{1,0:T(8,128)S(1)} %pad_add_fusion.info_ref, bf16[320,160]{1,0:T(8,128)(2,1)S(1)} %copy.139.mpo_ref, bf16[4,136,256]{2,1,0:T(8,128)(2,1)S(1)} %copy.140.tensor_ref, bf16[4,136,256]{2,1,0:T(8,128)(2,1)S(1)} %copy.141.far_tensor_ref, ...), custom_call_target="tpu_custom_call" | custom-call | tf_op jit(solution)/shard_map/expand_kernel/pallas_call | solution.py:297
  74.3 6.6 %all-to-all-start.3 = ((bf16[64,48,128]{2,1,0:T(8,128)(2,1)}), bf16[64,48,128]{2,1,0:T(8,128)(2,1)S(1)}, u32[]{:S(2)}, u32[]{:S(2)}) async-start(bf16[64,48,128]{2,1,0:T(8,128)(2,1)} %expand_kernel.18), calls=%async_computation.3 | async-start | bytes 1572864 | tf_op jit(solution)/shard_map/all_to_all | solution.py:46
  82.8 19.4 %all-to-all-done.3.inbox_ref = bf16[64,48,128]{2,1,0:T(8,128)(2,1)S(1)} async-done(((bf16[64,48,128]{2,1,0:T(8,128)(2,1)}), bf16[64,48,128]{2,1,0:T(8,128)(2,1)S(1)}, u32[]{:S(2)}, u32[]{:S(2)}) %all-to-all-start.3) | async-done | bytes 786464 | tf_op jit(solution)/shard_map/all_to_all | solution.py:46
  105.5 3.7 %expand_kernel.19 = bf16[64,48,128]{2,1,0:T(8,128)(2,1)S(1)} custom-call(s32[1]{0:T(128)} %constant.127.clone.1.step_ref, s32[9,256]{1,0:T(8,128)S(1)} %pad_add_fusion.info_ref, bf16[320,160]{1,0:T(8,128)(2,1)S(1)} %copy.139.mpo_ref, bf16[4,136,256]{2,1,0:T(8,128)(2,1)S(1)} %copy.140.tensor_ref, bf16[4,136,256]{2,1,0:T(8,128)(2,1)S(1)} %copy.141.far_tensor_ref, ...), custom_call_target="tpu_custom_call" | custom-call | tf_op jit(solution)/shard_map/expand_kernel/pallas_call | solution.py:297
  109.2 25.4 %all_to_all.42.inbox_ref = bf16[64,48,128]{2,1,0:T(8,128)(2,1)S(1)} all-to-all(bf16[64,48,128]{2,1,0:T(8,128)(2,1)S(1)} %expand_kernel.19), channel_id=1, replica_groups={{0,1,2,3,4,5,6,7,64,65,66,67,68,69,70,71,128,129,130,131,132,133,134,13..., dimensions={0} | all-to-all | bytes 1572864 | tf_op jit(solution)/shard_map/all_to_all | solution.py:46
  136.3 105.4 %while.17 = (s32[]{:T(128)}, bf16[8,48,128]{2,1,0:T(8,128)(2,1)S(1)}, bf16[2,8,48,128]{3,2,1,0:T(8,128)(2,1)S(1)}, s32[9,256]{1,0:T(8,128)S(1)}, bf16[320,160]{1...) while((s32[]{:T(128)}, ...), condition=%wide.region_3.4_spmd, body=%wide.region_2.3_spmd.sunk | while | flops 393223 | bytes 5505309 | solution.py:588
  137.7 3.7 %expand_kernel.20 = bf16[64,48,128]{2,1,0:T(8,128)(2,1)S(1)} custom-call(s32[1]{0:T(128)} %bitcast.68.step_ref, s32[9,256]{1,0:T(8,128)S(1)} %get-tuple-element.378.info_ref, bf16[320,160]{1,0:T(8,128)(2,1)S(1)} %get-tuple-element.379.mpo_ref, bf16[4,136,256]{2,1,0:T(8,128)(2,1)S(1)} %get-tuple-element.380.tensor_ref, ...), custom_call_target="tpu_custom_call" | custom-call | tf_op jit(solution)/shard_map/while/body/eval_jaxpr/expand_kernel/pallas_call | solution.py:297
  141.4 19.0 %all_to_all.46.inbox_ref = bf16[64,48,128]{2,1,0:T(8,128)(2,1)S(1)} all-to-all(bf16[64,48,128]{2,1,0:T(8,128)(2,1)S(1)} %expand_kernel.20), channel_id=1, replica_groups={{0,1,2,3,4,5,6,7,64,65,66,67,68,69,70,71,128,129,130,131,132,133,134,13..., dimensions={0} | all-to-all | bytes 1572864 | tf_op jit(solution)/shard_map/while/body/eval_jaxpr/all_to_all | solution.py:46
  163.6 4.6 %expand_kernel.21 = bf16[64,48,128]{2,1,0:T(8,128)(2,1)} custom-call(s32[1]{0:T(128)} %bitcast.67.step_ref, s32[9,256]{1,0:T(8,128)S(1)} %get-tuple-element.378.info_ref, bf16[320,160]{1,0:T(8,128)(2,1)S(1)} %get-tuple-element.379.mpo_ref, bf16[4,136,256]{2,1,0:T(8,128)(2,1)S(1)} %get-tuple-element.380.tensor_ref, ...), custom_call_target="tpu_custom_call" | custom-call | tf_op jit(solution)/shard_map/while/body/eval_jaxpr/expand_kernel/pallas_call | solution.py:297
  168.2 6.6 %all-to-all-start.1 = ((bf16[64,48,128]{2,1,0:T(8,128)(2,1)}), bf16[64,48,128]{2,1,0:T(8,128)(2,1)S(1)}, u32[]{:S(2)}, u32[]{:S(2)}) async-start(bf16[64,48,128]{2,1,0:T(8,128)(2,1)} %expand_kernel.21), calls=%async_computation.1 | async-start | bytes 1572864 | tf_op jit(solution)/shard_map/while/body/eval_jaxpr/all_to_all | solution.py:46
  174.9 12.4 %all-to-all-done.1.inbox_ref = bf16[64,48,128]{2,1,0:T(8,128)(2,1)S(1)} async-done(((bf16[64,48,128]{2,1,0:T(8,128)(2,1)}), bf16[64,48,128]{2,1,0:T(8,128)(2,1)S(1)}, u32[]{:S(2)}, u32[]{:S(2)}) %all-to-all-start.1) | async-done | bytes 786464 | tf_op jit(solution)/shard_map/while/body/eval_jaxpr/all_to_all | solution.py:46
  190.5 3.7 %expand_kernel.20 = bf16[64,48,128]{2,1,0:T(8,128)(2,1)S(1)} custom-call(s32[1]{0:T(128)} %bitcast.68.step_ref, s32[9,256]{1,0:T(8,128)S(1)} %get-tuple-element.378.info_ref, bf16[320,160]{1,0:T(8,128)(2,1)S(1)} %get-tuple-element.379.mpo_ref, bf16[4,136,256]{2,1,0:T(8,128)(2,1)S(1)} %get-tuple-element.380.tensor_ref, ...), custom_call_target="tpu_custom_call" | custom-call | tf_op jit(solution)/shard_map/while/body/eval_jaxpr/expand_kernel/pallas_call | solution.py:297
  194.2 18.9 %all_to_all.46.inbox_ref = bf16[64,48,128]{2,1,0:T(8,128)(2,1)S(1)} all-to-all(bf16[64,48,128]{2,1,0:T(8,128)(2,1)S(1)} %expand_kernel.20), channel_id=1, replica_groups={{0,1,2,3,4,5,6,7,64,65,66,67,68,69,70,71,128,129,130,131,132,133,134,13..., dimensions={0} | all-to-all | bytes 1572864 | tf_op jit(solution)/shard_map/while/body/eval_jaxpr/all_to_all | solution.py:46
  216.2 4.6 %expand_kernel.21 = bf16[64,48,128]{2,1,0:T(8,128)(2,1)} custom-call(s32[1]{0:T(128)} %bitcast.67.step_ref, s32[9,256]{1,0:T(8,128)S(1)} %get-tuple-element.378.info_ref, bf16[320,160]{1,0:T(8,128)(2,1)S(1)} %get-tuple-element.379.mpo_ref, bf16[4,136,256]{2,1,0:T(8,128)(2,1)S(1)} %get-tuple-element.380.tensor_ref, ...), custom_call_target="tpu_custom_call" | custom-call | tf_op jit(solution)/shard_map/while/body/eval_jaxpr/expand_kernel/pallas_call | solution.py:297
  220.8 6.6 %all-to-all-start.1 = ((bf16[64,48,128]{2,1,0:T(8,128)(2,1)}), bf16[64,48,128]{2,1,0:T(8,128)(2,1)S(1)}, u32[]{:S(2)}, u32[]{:S(2)}) async-start(bf16[64,48,128]{2,1,0:T(8,128)(2,1)} %expand_kernel.21), calls=%async_computation.1 | async-start | bytes 1572864 | tf_op jit(solution)/shard_map/while/body/eval_jaxpr/all_to_all | solution.py:46
  227.6 12.4 %all-to-all-done.1.inbox_ref = bf16[64,48,128]{2,1,0:T(8,128)(2,1)S(1)} async-done(((bf16[64,48,128]{2,1,0:T(8,128)(2,1)}), bf16[64,48,128]{2,1,0:T(8,128)(2,1)S(1)}, u32[]{:S(2)}, u32[]{:S(2)}) %all-to-all-start.1) | async-done | bytes 786464 | tf_op jit(solution)/shard_map/while/body/eval_jaxpr/all_to_all | solution.py:46
  243.1 2.3 start_kernel.1
  245.4 12.7 %all_to_all.43.got_ref = f32[32,1,128]{2,1,0:T(1,128)S(1)} all-to-all(f32[32,1,128]{2,1,0:T(1,128)S(1)} %get-tuple-element.223), channel_id=1, replica_groups={{0,1,2,3,4,5,6,7,64,65,66,67,68,69,70,71,128,129,130,131,132,133,134,13..., dimensions={0} | all-to-all | bytes 32768 | tf_op jit(solution)/shard_map/all_to_all | solution.py:46
  259.8 11.6 %all_to_all.44.got_ref = f32[32,1,128]{2,1,0:T(1,128)S(1)} all-to-all(f32[32,1,128]{2,1,0:T(1,128)S(1)} %get-tuple-element.228), channel_id=1, replica_groups={{0,1,2,3,4,5,6,7,64,65,66,67,68,69,70,71,128,129,130,131,132,133,134,13..., dimensions={0} | all-to-all | bytes 32768 | tf_op jit(solution)/shard_map/all_to_all | solution.py:46
  271.4 2.4 two_kernel.1
  273.8 11.6 %all_to_all.45.got_ref = f32[32,1,128]{2,1,0:T(1,128)S(1)} all-to-all(f32[32,1,128]{2,1,0:T(1,128)S(1)} %get-tuple-element.233), channel_id=1, replica_groups={{0,1,2,3,4,5,6,7,64,65,66,67,68,69,70,71,128,129,130,131,132,133,134,13..., dimensions={0} | all-to-all | bytes 32768 | tf_op jit(solution)/shard_map/all_to_all | solution.py:46
  286.3 2.8 collective-permute-start.13
  289.1 9.4 %collective-permute-done.13 = f32[40,256]{1,0:T(8,128)S(1)} collective-permute-done((f32[40,256]{1,0:T(8,128)S(1)}, f32[40,256]{1,0:T(8,128)S(1)}, u32[]{:S(2)}, u32[]{:S(2)}) %collective-permute-start.13) | collective-permute-done | bytes 40992 | tf_op jit(solution)/shard_map/ppermute | solution.py:39
  (110 shorter events, 43.6 us)
Async XLA Ops:
  0.6 17.9 %copy-start = (bf16[8,20,1024]{2,0,1:T(8,128)(2,1)S(1)}, bf16[8,20,1024]{2,0,1:T(8,128)(2,1)}, u32[]{:S(2)}) copy-start(bf16[8,20,1024]{2,0,1:T(8,128)(2,1)} %param.10) | copy-start | bytes 983044
  0.6 17.7 %copy-start.2 = (bf16[4,20,20]{2,0,1:T(4,128)(2,1)S(1)}, bf16[4,20,20]{2,0,1:T(4,128)(2,1)}, u32[]{:S(2)}) copy-start(bf16[4,20,20]{2,0,1:T(4,128)(2,1)} %param.11) | copy-start | bytes 9604
  5.3 24.6 %collective-permute-start.5 = (bf16[136,256]{1,0:T(8,128)(2,1)S(1)}, bf16[136,256]{1,0:T(8,128)(2,1)S(1)}, u32[]{:S(2)}, u32[]{:S(2)}) collective-permute-start(bf16[136,256]{1,0:T(8,128)(2,1)S(1)} %pad_maximum_fusion.2), channel_id=1, source_target_pairs={{0,24},{1,25},{2,26},{3,27},{4,28},{5,29},{6,30},{7,31},{8,88},{9,... | collective-permute-start | bytes 208904 | tf_op jit(solution)/shard_map/ppermute | solution.py:39
  8.4 21.6 %collective-permute-start.4 = (bf16[136,256]{1,0:T(8,128)(2,1)S(1)}, bf16[136,256]{1,0:T(8,128)(2,1)S(1)}, u32[]{:S(2)}, u32[]{:S(2)}) collective-permute-start(bf16[136,256]{1,0:T(8,128)(2,1)S(1)} %pad_maximum_fusion.2), channel_id=1, source_target_pairs={{0,16},{1,17},{2,18},{3,19},{4,20},{5,21},{6,22},{7,23},{8,80},{9,... | collective-permute-start | bytes 208904 | tf_op jit(solution)/shard_map/ppermute | solution.py:39
  12.0 18.1 %collective-permute-start.3 = (bf16[136,256]{1,0:T(8,128)(2,1)S(1)}, bf16[136,256]{1,0:T(8,128)(2,1)S(1)}, u32[]{:S(2)}, u32[]{:S(2)}) collective-permute-start(bf16[136,256]{1,0:T(8,128)(2,1)S(1)} %pad_maximum_fusion.2), channel_id=1, source_target_pairs={{0,8},{1,9},{2,10},{3,11},{4,12},{5,13},{6,14},{7,15},{8,72},{9,73... | collective-permute-start | bytes 208904 | tf_op jit(solution)/shard_map/ppermute | solution.py:39
  16.1 14.2 %collective-permute-start.2 = (bf16[136,256]{1,0:T(8,128)(2,1)S(1)}, bf16[136,256]{1,0:T(8,128)(2,1)S(1)}, u32[]{:S(2)}, u32[]{:S(2)}) collective-permute-start(bf16[136,256]{1,0:T(8,128)(2,1)S(1)} %pad_maximum_fusion.2), channel_id=1, source_target_pairs={{0,0},{1,1},{2,2},{3,3},{4,4},{5,5},{6,6},{7,7},{8,64},{9,65},{10,... | collective-permute-start | bytes 208904 | tf_op jit(solution)/shard_map/ppermute | solution.py:39
  19.9 13.8 %collective-permute-start.7 = (bf16[320,256]{1,0:T(8,128)(2,1)S(1)}, bf16[320,256]{1,0:T(8,128)(2,1)S(1)}, u32[]{:S(2)}, u32[]{:S(2)}) collective-permute-start(bf16[320,256]{1,0:T(8,128)(2,1)S(1)} %reshape.92), channel_id=1, source_target_pairs={{0,0},{1,1},{2,2},{3,3},{4,4},{5,5},{6,6},{7,7},{8,64},{9,65},{10,... | collective-permute-start | bytes 491528 | tf_op jit(solution)/shard_map/ppermute | solution.py:39
  31.0 2.7 collective-permute-start.6
  33.7 1.4 collective-permute-start.8
  33.8 20.3 %copy-start.4 = (s32[8]{0:T(128)S(1)}, s32[8]{0:T(128)}, u32[]{:S(2)}) copy-start(s32[8]{0:T(128)} %param.15) | copy-start | bytes 100
  33.8 20.5 %copy-start.3 = (bf16[1,8,1024]{2,1,0:T(8,128)(2,1)S(1)}, bf16[1,8,1024]{2,1,0:T(8,128)(2,1)}, u32[]{:S(2)}) copy-start(bf16[1,8,1024]{2,1,0:T(8,128)(2,1)} %param.16) | copy-start | bytes 49156
  33.8 20.7 %copy-start.1 = (bf16[1,8,20,1024]{3,1,2,0:T(8,128)(2,1)S(1)}, bf16[1,8,20,1024]{3,1,2,0:T(8,128)(2,1)}, u32[]{:S(2)}) copy-start(bf16[1,8,20,1024]{3,1,2,0:T(8,128)(2,1)} %param.17) | copy-start | bytes 983044
  39.2 27.3 %all-to-all-start.2 = ((bf16[64,48,128]{2,1,0:T(8,128)(2,1)}), bf16[64,48,128]{2,1,0:T(8,128)(2,1)S(1)}, u32[]{:S(2)}, u32[]{:S(2)}) async-start(bf16[64,48,128]{2,1,0:T(8,128)(2,1)} %first_kernel.1), calls=%async_computation.2 | async-start | bytes 1572864 | tf_op jit(solution)/shard_map/all_to_all | solution.py:46
  68.3 1.4 collective-permute-start.9
  74.3 28.0 %all-to-all-start.3 = ((bf16[64,48,128]{2,1,0:T(8,128)(2,1)}), bf16[64,48,128]{2,1,0:T(8,128)(2,1)S(1)}, u32[]{:S(2)}, u32[]{:S(2)}) async-start(bf16[64,48,128]{2,1,0:T(8,128)(2,1)} %expand_kernel.18), calls=%async_computation.3 | async-start | bytes 1572864 | tf_op jit(solution)/shard_map/all_to_all | solution.py:46
  80.9 24.5 %collective-permute-start.11 = (bf16[680,256]{1,0:T(8,128)(2,1)S(1)}, bf16[680,256]{1,0:T(8,128)(2,1)S(1)}, u32[]{:S(2)}, u32[]{:S(2)}) collective-permute-start(bf16[680,256]{1,0:T(8,128)(2,1)S(1)} %pad_maximum_fusion), channel_id=1, source_target_pairs={{0,0},{1,1},{2,2},{3,3},{4,4},{5,5},{6,6},{7,7},{8,64},{9,65},{10,... | collective-permute-start | bytes 1044488 | tf_op jit(solution)/shard_map/ppermute | solution.py:39
  104.0 1.4 collective-permute-start.10
  136.3 1.4 collective-permute-start
  162.2 1.4 collective-permute-start.1
  168.2 19.1 %all-to-all-start.1 = ((bf16[64,48,128]{2,1,0:T(8,128)(2,1)}), bf16[64,48,128]{2,1,0:T(8,128)(2,1)S(1)}, u32[]{:S(2)}, u32[]{:S(2)}) async-start(bf16[64,48,128]{2,1,0:T(8,128)(2,1)} %expand_kernel.21), calls=%async_computation.1 | async-start | bytes 1572864 | tf_op jit(solution)/shard_map/while/body/eval_jaxpr/all_to_all | solution.py:46
  189.1 1.4 collective-permute-start
  214.8 1.4 collective-permute-start.1
  220.8 19.1 %all-to-all-start.1 = ((bf16[64,48,128]{2,1,0:T(8,128)(2,1)}), bf16[64,48,128]{2,1,0:T(8,128)(2,1)S(1)}, u32[]{:S(2)}, u32[]{:S(2)}) async-start(bf16[64,48,128]{2,1,0:T(8,128)(2,1)} %expand_kernel.21), calls=%async_computation.1 | async-start | bytes 1572864 | tf_op jit(solution)/shard_map/while/body/eval_jaxpr/all_to_all | solution.py:46
  241.7 1.4 collective-permute-start.12
  286.3 12.2 %collective-permute-start.13 = (f32[40,256]{1,0:T(8,128)S(1)}, f32[40,256]{1,0:T(8,128)S(1)}, u32[]{:S(2)}, u32[]{:S(2)}) collective-permute-start(f32[40,256]{1,0:T(8,128)S(1)} %last_kernel.1), channel_id=1, source_target_pairs={{0,0},{1,1},{2,2},{3,3},{4,4},{5,5},{6,6},{7,7},{8,64},{9,65},{10,... | collective-permute-start | bytes 122888 | tf_op jit(solution)/shard_map/ppermute | solution.py:39
